TPU v7x, 256 devices: a whole 4x4x8 slice. The times are simulated.
256 devices in a mesh: pb: 8 (over x, y_hi), ka: 32 (over y_lo, z, core).
Axes of the slice: x: 4, y: 4 (y_hi: 2, y_lo: 2; y = y_hi * 2 + y_lo), z: 8, core: 2. Of those that a mesh axis runs over, the one named last changes fastest.
Arguments:
- queries: bfloat16 [32768, 2048], P(('pb', 'ka')), may hold values from -3 to 3
- keys: bfloat16 [32768, 2048], P(('pb', 'ka')), may hold values from -3 to 3
- values: bfloat16 [32768, 2048], P(('pb', 'ka')), may hold values from -3 to 3
- outputs: bfloat16 [32768, 2048], P(('pb', 'ka')), may hold values from -3 to 3
- d_out: bfloat16 [32768, 2048], P(('pb', 'ka')), may hold values from -16 to 16
- row_lse: float32 [16, 32768], P(None, ('pb', 'ka')), may hold values from 6.5 to 8.5
- adjacency: int32 [256, 2, 4, 1], P(('pb', 'ka')), may hold values from 0 to 1, as said below
Outputs:
- grad_queries: bfloat16 [32768, 2048], P(('pb', 'ka'))
- grad_keys: bfloat16 [32768, 2048], P(('pb', 'ka'))
- grad_values: bfloat16 [32768, 2048], P(('pb', 'ka'))
Inputs may be any that keep to these rules, and one draw needn't show every extreme that they name: 1 where the query block attends that key block of its window, else 0; every query block attends its own key block, adjacency[b, 0, 0, 0] = 1.
All inputs are finite; a program needn't handle non-finite values.
Results may differ from a plain program's by a relative error of at most 0.0075.
Values may be sent and summed in bfloat16 or wider, within the bound.
No kernel may reach another device: no remote copies, remote signals or barrier semaphores. Data moves between devices by JAX's collectives and lax.ppermute only.
A program may use at most 128 MiB of HBM per device.

v0:
```python
import functools
import math

import jax
import jax.numpy as jnp
from jax import lax
from jax.experimental import pallas as pl
from jax.experimental.pallas import tpu as pltpu
from jax.sharding import PartitionSpec as P

HEAD_DIM = 128
BLOCK = 128
WINDOW = 4
STAT = 16
HALF = 8
QROWS = 2 * BLOCK + STAT
KROWS = 2 * BLOCK
LOG2E = math.log2(math.e)
SCALE = 1.0 / math.sqrt(HEAD_DIM)
FAR_AWAY = 1e30
F32 = jnp.float32
BF16 = jnp.bfloat16


def three_pieces(value):
    high = value.astype(BF16).astype(F32)
    rest = value - high
    middle = rest.astype(BF16).astype(F32)
    return high, middle, rest - middle


def pack_head(adj_ref, g, o, lse_row):
    down = lax.broadcasted_iota(jnp.int32, (BLOCK, BLOCK), 0)
    across = lax.broadcasted_iota(jnp.int32, (BLOCK, BLOCK), 1)
    product = contract(o, g, 1, 1)
    delta_row = jnp.sum(jnp.where(down == across, product, 0.0), axis=0, keepdims=True)
    rows = list(three_pieces(lse_row)) + list(three_pieces(delta_row))
    line = lax.broadcasted_iota(jnp.int32, (STAT, BLOCK), 0)
    stat = jnp.zeros((STAT, BLOCK), F32)
    for i, row in enumerate(rows):
        stat = jnp.where(line == i, jnp.broadcast_to(row, (STAT, BLOCK)), stat)
    for i in range(2 * WINDOW):
        flag = (adj_ref[0, i // WINDOW, i % WINDOW, 0] == 1).astype(jnp.int32).astype(F32)
        stat = jnp.where(line == 8 + i, flag, stat)
    return stat.astype(BF16)


def contract(a, b, da, db):
    return lax.dot_general(a, b, (((da,), (db,)), ((), ())), preferred_element_type=F32)


def unpack_stat(stat, row, slot_flag):
    stat = stat.astype(F32)
    lse = stat[0:1] + stat[1:2] + stat[2:3]
    delta = stat[3:4] + stat[4:5] + stat[5:6]
    keep = slot_flag(stat, 8 + WINDOW * row) > 0.5
    return jnp.where(keep, lse * LOG2E, FAR_AWAY), delta


def flag_of(w):
    return lambda stat, base: stat[base + w:base + w + 1]


def flag_by_parity(odd, w_even, w_odd):
    return lambda stat, base: jnp.where(
        odd == 1, stat[base + w_odd:base + w_odd + 1], stat[base + w_even:base + w_even + 1])


def terms(q, g, k, v, lse, delta):
    scores = contract(k, q, 1, 1) * (SCALE * LOG2E)
    prob = jnp.exp2(scores - lse)
    grad = prob * (contract(v, g, 1, 1) - delta)
    low = prob.astype(BF16)
    grad = grad.astype(BF16)
    dv = contract(low, g, 1, 0)
    dk = contract(grad, q, 1, 0) * SCALE
    dq = contract(grad, k, 0, 0) * SCALE
    return dq, dk, dv

def vmem(shape, dtype):
    return pltpu.VMEM(shape, dtype)


def on_chip(value):
    return pltpu.with_memory_space_constraint(value, pltpu.VMEM)


def call_on_chip(kernel, name, odd, inputs, outs, flops, exps=0, after=None):
    spec = pl.BlockSpec(memory_space=pltpu.VMEM)
    moved_bytes = sum(x.size * x.dtype.itemsize for x in inputs)
    return pl.pallas_call(
        kernel,
        in_specs=[pl.BlockSpec(memory_space=pltpu.SMEM)] + [spec] * len(inputs),
        out_specs=[spec] * len(outs),
        out_shape=[vmem(s, t) for s, t in outs],
        compiler_params=pltpu.CompilerParams(vmem_limit_bytes=16 * 2**20),
        cost_estimate=pl.CostEstimate(flops=flops, bytes_accessed=moved_bytes, transcendentals=exps),
        name=name,
    )(odd, *[on_chip(x) for x in inputs])


def arrived_kernel(odd_ref, *refs):
    refs[-1][0] = odd_ref[0]


def arrived(odd, *inputs):
    spec = pl.BlockSpec(memory_space=pltpu.VMEM)
    smem = pl.BlockSpec(memory_space=pltpu.SMEM)
    return pl.pallas_call(
        arrived_kernel,
        in_specs=[smem] + [spec] * len(inputs),
        out_specs=smem,
        out_shape=jax.ShapeDtypeStruct((1,), jnp.int32),
        compiler_params=pltpu.CompilerParams(vmem_limit_bytes=2**20),
        cost_estimate=pl.CostEstimate(flops=WAIT_FLOPS, bytes_accessed=2**20, transcendentals=0),
        name="arrived",
    )(odd, *[on_chip(x) for x in inputs])


WAIT_FLOPS = 10**11
PACK_STEP = 4


def pack_kernel(odd_ref, adj_ref, lse_ref, q_hbm, k_hbm, v_hbm, o_hbm, g_hbm,
                xqa, xka, xqb, xkb, cross, q_in, k_in, v_in, o_in, g_in, sems):
    width = PACK_STEP * HEAD_DIM
    chunks = 2 * HALF // PACK_STEP
    copies = []
    for c in range(chunks):
        cols = pl.ds(c * width, width)
        copies.append([
            pltpu.make_async_copy(a.at[:, cols], b.at[:, cols], sems.at[c, i])
            for i, (a, b) in enumerate(
                [(q_hbm, q_in), (g_hbm, g_in), (o_hbm, o_in), (k_hbm, k_in), (v_hbm, v_in)])])
        for copy in copies[c]:
            copy.start()
    for c in range(chunks):
        for copy in copies[c]:
            copy.wait()
        for head in range(c * PACK_STEP, (c + 1) * PACK_STEP):
            cols = slice(head * HEAD_DIM, (head + 1) * HEAD_DIM)
            h = head % HALF
            xq, xk = (xqa, xka) if head < HALF else (xqb, xkb)
            xq[h, 0:128, :] = q_in[:, cols]
            xq[h, 128:256, :] = g_in[:, cols]
            xq[h, 256:272, :] = pack_head(adj_ref, g_in[:, cols], o_in[:, cols], lse_ref[head:head + 1])
            xk[h, 0:128, :] = k_in[:, cols]
            xk[h, 128:256, :] = v_in[:, cols]

    is_odd = odd_ref[0] == 1

    @pl.when(is_odd)
    def _():
        cross[...] = xqa[...]

    @pl.when(jnp.logical_not(is_odd))
    def _():
        cross[:, 0:KROWS, :] = xkb[...]
        cross[:, KROWS:QROWS, :] = jnp.zeros((HALF, STAT, HEAD_DIM), BF16)


def pack(odd, adjacency, queries, keys, values, outputs, d_out, row_lse):
    smem = pl.BlockSpec(memory_space=pltpu.SMEM)
    spec = pl.BlockSpec(memory_space=pltpu.VMEM)
    anywhere = pl.BlockSpec(memory_space=pltpu.HBM)
    shapes = [QROWS, KROWS, QROWS, KROWS, QROWS]
    return pl.pallas_call(
        pack_kernel,
        in_specs=[smem, smem, spec] + [anywhere] * 5,
        out_specs=[spec] * len(shapes),
        out_shape=[vmem((HALF, s, HEAD_DIM), BF16) for s in shapes],
        scratch_shapes=[pltpu.VMEM((BLOCK, 2 * HALF * HEAD_DIM), BF16)] * 5
        + [pltpu.SemaphoreType.DMA((2 * HALF // PACK_STEP, 5))],
        compiler_params=pltpu.CompilerParams(vmem_limit_bytes=16 * 2**20),
        cost_estimate=pl.CostEstimate(flops=10**8, bytes_accessed=5 * 2**20, transcendentals=0),
        name="pack",
    )(odd, adjacency, row_lse, *[pltpu.with_memory_space_constraint(x, pltpu.HBM)
                                 for x in (queries, keys, values, outputs, d_out)])


Q3 = slice(0, QROWS)
K3 = slice(QROWS, QROWS + KROWS)
NEAR_Q = slice(QROWS + KROWS, 2 * QROWS + KROWS)
NEAR_K = slice(QROWS + KROWS, QROWS + 2 * KROWS)
MATE_ROWS = 2 * QROWS + KROWS


def mates_kernel(odd_ref, xqa, xkb, q2, k2, out):
    def one_head(h, carry):
        out[h, Q3] = q2[h]
        out[h, K3] = k2[h]
        return carry

    lax.fori_loop(0, HALF, one_head, 0)
    is_odd = odd_ref[0] == 1

    @pl.when(is_odd)
    def _():
        out[:, NEAR_K, :] = xkb[...]
        out[:, NEAR_K.stop:, :] = jnp.zeros((HALF, STAT, HEAD_DIM), BF16)

    @pl.when(jnp.logical_not(is_odd))
    def _():
        out[:, NEAR_Q, :] = xqa[...]


def attend_a_kernel(odd_ref, xqa, cross, q2, mates, xka, fk, swap_b,
                    q_own, q_two, kv_own, swap_out, down_out, far_out):
    odd = odd_ref[0]
    is_odd = odd == 1
    flags = [flag_of(0), flag_by_parity(odd, 3, 1), flag_of(2), flag_by_parity(odd, 1, 3)]

    def one_head(h, carry):
        slots = [xqa[h], jnp.where(is_odd, mates[h, NEAR_Q], cross[h]), q2[h], mates[h, Q3]]
        q = jnp.concatenate([s[0:128] for s in slots], axis=0)
        g = jnp.concatenate([s[128:256] for s in slots], axis=0)
        lse = []
        for row in range(2):
            both = [unpack_stat(s[256:272], row, f) for s, f in zip(slots, flags)]
            lse.append(jnp.broadcast_to(jnp.concatenate([b[0] for b in both], axis=1), (128, 512)))
            delta = jnp.concatenate([b[1] for b in both], axis=1)
        k = jnp.concatenate([xka[h, 0:128], fk[h, 0:128]], axis=0)
        v = jnp.concatenate([xka[h, 128:256], fk[h, 128:256]], axis=0)
        dq, dk, dv = terms(q, g, k, v, jnp.concatenate(lse, axis=0), delta)
        q_own[h] = dq[0:128]
        down_out[h] = dq[128:256].astype(BF16)
        q_two[h] = dq[256:384]
        swap_out[h, 0:128] = dq[384:512].astype(BF16)
        swap_out[h, 128:384] = swap_b[h]
        kv_own[h, 0:128] = dk[0:128]
        kv_own[h, 128:256] = dv[0:128]
        far_out[h, 0:128] = dk[128:256].astype(BF16)
        far_out[h, 128:256] = dv[128:256].astype(BF16)
        return carry

    lax.fori_loop(0, HALF, one_head, 0)


def attend_b_kernel(odd_ref, xkb, cross, k2, mates, xqb, fq,
                    kv_own, kv_two, q_own, swap_out, up_out, far_out):
    odd = odd_ref[0]
    is_odd = odd == 1
    flags = [flag_of(0), flag_by_parity(odd, 1, 3), flag_of(2), flag_by_parity(odd, 3, 1)]

    def one_head(h, carry):
        slots = [xkb[h], jnp.where(is_odd, cross[h, 0:KROWS], mates[h, NEAR_K]), k2[h], mates[h, K3]]
        k = jnp.concatenate([s[0:128] for s in slots], axis=0)
        v = jnp.concatenate([s[128:256] for s in slots], axis=0)
        q = jnp.concatenate([xqb[h, 0:128], fq[h, 0:128]], axis=0)
        g = jnp.concatenate([xqb[h, 128:256], fq[h, 128:256]], axis=0)
        stat_own, stat_far = xqb[h, 256:272], fq[h, 256:272]
        lse = []
        for f in flags:
            own, own_delta = unpack_stat(stat_own, 0, f)
            far, far_delta = unpack_stat(stat_far, 1, f)
            lse.append(jnp.broadcast_to(jnp.concatenate([own, far], axis=1), (128, 256)))
            delta = jnp.concatenate([own_delta, far_delta], axis=1)
        dq, dk, dv = terms(q, g, k, v, jnp.concatenate(lse, axis=0), delta)
        q_own[h] = dq[0:128]
        far_out[h] = dq[128:256].astype(BF16)
        kv_own[h, 0:128] = dk[0:128]
        kv_own[h, 128:256] = dv[0:128]
        up_out[h, 0:128] = dk[128:256].astype(BF16)
        up_out[h, 128:256] = dv[128:256].astype(BF16)
        kv_two[h, 0:128] = dk[256:384]
        kv_two[h, 128:256] = dv[256:384]
        swap_out[h, 0:128] = dk[384:512].astype(BF16)
        swap_out[h, 128:256] = dv[384:512].astype(BF16)
        return carry

    lax.fori_loop(0, HALF, one_head, 0)


def block(rows, dtype):
    return ((HALF, rows, HEAD_DIM), dtype)


def attend_a(odd, *inputs):
    outs = [block(128, F32), block(128, F32), block(256, F32), block(384, BF16), block(128, BF16), block(256, BF16)]
    return call_on_chip(attend_a_kernel, "attend_a", odd, inputs, outs, 13 * 10**8, 2**20)


def attend_b(odd, *inputs):
    outs = [block(256, F32), block(256, F32), block(128, F32), block(256, BF16), block(256, BF16), block(128, BF16)]
    return call_on_chip(attend_b_kernel, "attend_b", odd, inputs, outs, 13 * 10**8, 2**20)


def combine_kernel(parity, rows, odd_ref, mine, swapped, relayed_in, total):
    taken = odd_ref[0] == parity

    def one_head(h, carry):
        relay = jnp.where(taken, relayed_in[h].astype(F32), 0.0)
        total[h] = (mine[h] + swapped[h, rows].astype(F32) + relay).astype(BF16)
        return carry

    lax.fori_loop(0, HALF, one_head, 0)


def combine(parity, rows, name, odd, *inputs):
    return call_on_chip(functools.partial(combine_kernel, parity, rows), name, odd, inputs,
                        [(inputs[0].shape, BF16)], 10**6)[0]


def finish_kernel(odd_ref, q_own, kv_a, down, down_sum, far_k, k_own, q_b, up, up_sum, far_q,
                  dq_hbm, dk_hbm, dv_hbm, dq, dk, dv, sems):
    odd = odd_ref[0]
    copies = []
    for head in range(2 * HALF):
        h = head % HALF
        cols = slice(head * HEAD_DIM, (head + 1) * HEAD_DIM)
        if head < HALF:
            from_down = jnp.where(odd == 1, 0.0, down[h].astype(F32))
            grad_q = q_own[h] + down_sum[h].astype(F32) + from_down
            grad_kv = kv_a[h] + far_k[h].astype(F32)
        else:
            from_up = jnp.where(odd == 1, up[h].astype(F32), 0.0)
            grad_q = q_b[h] + far_q[h].astype(F32)
            grad_kv = k_own[h] + up_sum[h].astype(F32) + from_up
        dq[:, cols] = grad_q.astype(BF16)
        dk[:, cols] = grad_kv[0:128].astype(BF16)
        dv[:, cols] = grad_kv[128:256].astype(BF16)
        if head % PACK_STEP == PACK_STEP - 1:
            c = head // PACK_STEP
            span = pl.ds(c * PACK_STEP * HEAD_DIM, PACK_STEP * HEAD_DIM)
            for i, (a, b) in enumerate([(dq, dq_hbm), (dk, dk_hbm), (dv, dv_hbm)]):
                copies.append(pltpu.make_async_copy(a.at[:, span], b.at[:, span], sems.at[c, i]))
                copies[-1].start()
    for copy in copies:
        copy.wait()


def finish(odd, *inputs):
    spec = pl.BlockSpec(memory_space=pltpu.VMEM)
    whole = (BLOCK, 2 * HALF * HEAD_DIM)
    return pl.pallas_call(
        finish_kernel,
        in_specs=[pl.BlockSpec(memory_space=pltpu.SMEM)] + [spec] * len(inputs),
        out_specs=[pl.BlockSpec(memory_space=pl.ANY)] * 3,
        out_shape=[jax.ShapeDtypeStruct(whole, BF16)] * 3,
        scratch_shapes=[pltpu.VMEM(whole, BF16)] * 3 + [pltpu.SemaphoreType.DMA((2 * HALF // PACK_STEP, 3))],
        compiler_params=pltpu.CompilerParams(vmem_limit_bytes=16 * 2**20),
        cost_estimate=pl.CostEstimate(flops=10**6, bytes_accessed=6 * 2**20, transcendentals=0),
        name="finish",
    )(odd, *[on_chip(x) for x in inputs])


def moved(value, axis, steps):
    count = lax.axis_size(axis)
    return lax.ppermute(value, axis, [(i, (i + steps) % count) for i in range(count)])


def exchanged(value):
    count = lax.axis_size("ka")
    return lax.ppermute(value, "ka", [(i, i ^ 1) for i in range(count)])


def crossed(value):
    count = lax.axis_size("ka")
    return lax.ppermute(value, "ka", [(i, (i + (3 if i % 2 == 1 else -3)) % count) for i in range(count)])


def local(queries, keys, values, outputs, d_out, row_lse, adjacency):
    odd = (lax.axis_index("ka") % 2).astype(jnp.int32).reshape(1)
    xqa, xka, xqb, xkb, cross = pack(odd, adjacency, queries, keys, values, outputs, d_out, row_lse)
    q2 = moved(xqa, "ka", 2)
    k2 = moved(xkb, "ka", -2)
    fq = moved(xqb, "pb", 1)
    fk = moved(xka, "pb", -1)
    cross = crossed(cross)
    mates = exchanged(call_on_chip(mates_kernel, "mates", odd, (xqa, xkb, q2, k2), [block(MATE_ROWS, BF16)], 10**5)[0])
    here = arrived(odd, fq, fk, cross)
    k_own, k_two, q_b, swap_b, up, far_q = attend_b(here, xkb, cross, k2, mates, xqb, fq)
    up = moved(up, "ka", 1)
    far_q = moved(far_q, "pb", -1)
    q_own, q_two, kv_a, swap, down, far_k = attend_a(here, xqa, cross, q2, mates, xka, fk, swap_b)
    down = moved(down, "ka", -1)
    swap = exchanged(swap)
    far_k = moved(far_k, "pb", 1)
    up_sum = moved(combine(0, slice(128, 384), "combine_b", odd, k_two, swap, up), "ka", 2)
    down_sum = moved(combine(1, slice(0, 128), "combine_a", odd, q_two, swap, down), "ka", -2)
    here = arrived(odd, far_q, far_k)
    return tuple(finish(here, q_own, kv_a, down, down_sum, far_k, k_own, q_b, up, up_sum, far_q))


def solution(mesh):
    rows = P(("pb", "ka"), None)
    placed = (rows, rows, rows, rows, rows, P(None, ("pb", "ka")), P(("pb", "ka"), None, None, None))
    return jax.shard_map(
        local,
        mesh=mesh,
        in_specs=placed,
        out_specs=(rows, rows, rows),
        check_vma=False,
    )
```

profile of v0, /device:TPU:1, one launch (start us, length us, event | category | flops | bytes accessed | tf_op | source)
XLA Modules:
  0.0 109.8 jit_solution(627217528177928240)
XLA Ops:
  0.6 0.8 copy.10.adj_ref
  1.4 0.0 copy-start
  1.4 0.7 copy-done
  2.1 3.2 %pack.1 = (bf16[8,272,128]{2,1,0:T(8,128)(2,1)S(1)}, bf16[8,256,128]{2,1,0:T(8,128)(2,1)S(1)}, bf16[8,272,128]{2,1,0:T(8,128)(2,1)S(1)}, bf16[8,256,128]{2,1,0:T(8,128)(2,1)S(1)}, bf16[8,272,128]{2,1,0:T(8,128)(2,1)S(1)}) custom-call(s32[1]{0:T(128)} %bitcast.odd_ref, s32[1,2,4,1]{3,2,1,0:T(4,128)S(1)} %copy.10.adj_ref, f32[16,128]{1,0:T(8,128)S(1)} %copy-done, ...), custom_call_target="tpu_custom_call" | custom-call | flops 100000000 | bytes 5242880 | tf_op jit(solution)/shard_map/pack/pallas_call | solution.py:167
  5.3 2.5 %collective-permute-start.4 = (bf16[8,272,128]{2,1,0:T(8,128)(2,1)S(1)}, bf16[8,272,128]{2,1,0:T(8,128)(2,1)S(1)}, u32[]{:S(2)}, u32[]{:S(2)}) collective-permute-start(bf16[8,272,128]{2,1,0:T(8,128)(2,1)S(1)} %get-tuple-element.24.xqa), channel_id=1, source_target_pairs={{0,2},{1,3},{2,4},{3,5},{4,6},{5,7},{6,8},{7,9},{8,10},{9,11},{10,... | collective-permute-start | bytes 1671176 | tf_op jit(solution)/shard_map/ppermute | solution.py:349
  7.9 3.9 %collective-permute-start.2 = (bf16[8,272,128]{2,1,0:T(8,128)(2,1)S(1)}, bf16[8,272,128]{2,1,0:T(8,128)(2,1)S(1)}, u32[]{:S(2)}, u32[]{:S(2)}) collective-permute-start(bf16[8,272,128]{2,1,0:T(8,128)(2,1)S(1)} %get-tuple-element.22), channel_id=1, source_target_pairs={{0,29},{1,4},{2,31},{3,6},{4,1},{5,8},{6,3},{7,10},{8,5},{9,12},{1... | collective-permute-start | bytes 1671176 | tf_op jit(solution)/shard_map/ppermute | solution.py:359
  11.7 2.9 %collective-permute-start = (bf16[8,272,128]{2,1,0:T(8,128)(2,1)S(1)}, bf16[8,272,128]{2,1,0:T(8,128)(2,1)S(1)}, u32[]{:S(2)}, u32[]{:S(2)}) collective-permute-start(bf16[8,272,128]{2,1,0:T(8,128)(2,1)S(1)} %get-tuple-element.20.xqb), channel_id=1, source_target_pairs={{0,32},{32,64},{64,96},{96,128},{128,160},{160,192},{192,224},{224... | collective-permute-start | bytes 1671176 | tf_op jit(solution)/shard_map/ppermute | solution.py:349
  14.6 1.3 %collective-permute-start.3 = (bf16[8,256,128]{2,1,0:T(8,128)(2,1)S(1)}, bf16[8,256,128]{2,1,0:T(8,128)(2,1)S(1)}, u32[]{:S(2)}, u32[]{:S(2)}) collective-permute-start(bf16[8,256,128]{2,1,0:T(8,128)(2,1)S(1)} %get-tuple-element.23.xkb), channel_id=1, source_target_pairs={{0,30},{1,31},{2,0},{3,1},{4,2},{5,3},{6,4},{7,5},{8,6},{9,7},{10,... | collective-permute-start | bytes 1572872 | tf_op jit(solution)/shard_map/ppermute | solution.py:349
  16.0 3.4 %collective-permute-start.1 = (bf16[8,256,128]{2,1,0:T(8,128)(2,1)S(1)}, bf16[8,256,128]{2,1,0:T(8,128)(2,1)S(1)}, u32[]{:S(2)}, u32[]{:S(2)}) collective-permute-start(bf16[8,256,128]{2,1,0:T(8,128)(2,1)S(1)} %get-tuple-element.21.xka), channel_id=1, source_target_pairs={{0,224},{32,0},{64,32},{96,64},{128,96},{160,128},{192,160},{224,1... | collective-permute-start | bytes 1572872 | tf_op jit(solution)/shard_map/ppermute | solution.py:349
  19.3 16.1 %collective-permute-done.3.k2 = bf16[8,256,128]{2,1,0:T(8,128)(2,1)S(1)} collective-permute-done((bf16[8,256,128]{2,1,0:T(8,128)(2,1)S(1)}, bf16[8,256,128]{2,1,0:T(8,128)(2,1)S(1)}, u32[]{:S(2)}, u32[]{:S(2)}) %collective-permute-start.3) | collective-permute-done | bytes 524320 | tf_op jit(solution)/shard_map/ppermute | solution.py:349
  35.5 0.0 collective-permute-done.4.q2
  35.5 0.1 mates.1
  35.6 8.9 %collective-permute-start.5 = (bf16[8,800,128]{2,1,0:T(8,128)(2,1)S(1)}, bf16[8,800,128]{2,1,0:T(8,128)(2,1)S(1)}, u32[]{:S(2)}, u32[]{:S(2)}) collective-permute-start(bf16[8,800,128]{2,1,0:T(8,128)(2,1)S(1)} %mates.1), channel_id=1, source_target_pairs={{0,1},{1,0},{2,3},{3,2},{4,5},{5,4},{6,7},{7,6},{8,9},{9,8},{10,11... | collective-permute-start | bytes 4915208 | tf_op jit(solution)/shard_map/ppermute | solution.py:354
  44.5 12.1 %collective-permute-done.1.refs_1_.fk = bf16[8,256,128]{2,1,0:T(8,128)(2,1)S(1)} collective-permute-done((bf16[8,256,128]{2,1,0:T(8,128)(2,1)S(1)}, bf16[8,256,128]{2,1,0:T(8,128)(2,1)S(1)}, u32[]{:S(2)}, u32[]{:S(2)}) %collective-permute-start.1) | collective-permute-done | bytes 524320 | tf_op jit(solution)/shard_map/ppermute | solution.py:349
  56.7 0.0 collective-permute-done.2.refs_2_.cross
  56.7 0.0 collective-permute-done.refs_0_.fq
  56.7 0.5 arrived.2.odd_ref
  57.2 0.0 collective-permute-done.5.mates
  57.2 5.2 %attend_b.1 = (f32[8,256,128]{2,1,0:T(8,128)S(1)}, f32[8,256,128]{2,1,0:T(8,128)S(1)}, f32[8,128,128]{2,1,0:T(8,128)S(1)}, bf16[8,256,128]{2,1,0:T(8,128)(2,1)S(...) custom-call(s32[1]{0:T(128)} %arrived.2.odd_ref, bf16[8,256,128]{2,1,0:T(8,128)(2,1)S(1)} %get-tuple-element.23.xkb, ...), custom_call_target="tpu_custom_call" | custom-call | flops 1300000000 | bytes 4358144 | tf_op jit(solution)/shard_map/attend_b/pallas_call | solution.py:91
  62.4 5.5 %attend_a.1 = (f32[8,128,128]{2,1,0:T(8,128)S(1)}, f32[8,128,128]{2,1,0:T(8,128)S(1)}, f32[8,256,128]{2,1,0:T(8,128)S(1)}, bf16[8,384,128]{2,1,0:T(8,128)(2,1)S(...) custom-call(s32[1]{0:T(128)} %arrived.2.odd_ref, bf16[8,272,128]{2,1,0:T(8,128)(2,1)S(1)} %get-tuple-element.24.xqa, ...), custom_call_target="tpu_custom_call" | custom-call | flops 1300000000 | bytes 4882432 | tf_op jit(solution)/shard_map/attend_a/pallas_call | solution.py:91
  67.9 0.6 collective-permute-start.9
  68.4 0.0 collective-permute-start.11
  68.4 0.1 collective-permute-start.7
  68.5 0.8 collective-permute-start.8
  69.3 5.0 %collective-permute-start.6 = (bf16[8,128,128]{2,1,0:T(8,128)(2,1)S(1)}, bf16[8,128,128]{2,1,0:T(8,128)(2,1)S(1)}, u32[]{:S(2)}, u32[]{:S(2)}) collective-permute-start(bf16[8,128,128]{2,1,0:T(8,128)(2,1)S(1)} %get-tuple-element.25), channel_id=1, source_target_pairs={{0,224},{32,0},{64,32},{96,64},{128,96},{160,128},{192,160},{224,1... | collective-permute-start | bytes 786440 | tf_op jit(solution)/shard_map/ppermute | solution.py:349
  74.3 0.3 collective-permute-done.8.relayed_in.down
  74.6 0.0 collective-permute-done.9.swapped
  74.6 0.1 combine_a.1
  74.7 6.9 %collective-permute-start.10 = (bf16[8,128,128]{2,1,0:T(8,128)(2,1)S(1)}, bf16[8,128,128]{2,1,0:T(8,128)(2,1)S(1)}, u32[]{:S(2)}, u32[]{:S(2)}) collective-permute-start(bf16[8,128,128]{2,1,0:T(8,128)(2,1)S(1)} %combine_a.1), channel_id=1, source_target_pairs={{0,30},{1,31},{2,0},{3,1},{4,2},{5,3},{6,4},{7,5},{8,6},{9,7},{10,... | collective-permute-start | bytes 786440 | tf_op jit(solution)/shard_map/ppermute | solution.py:349
  81.7 0.0 collective-permute-done.11.relayed_in.up
  81.7 0.2 combine_b.1
  81.9 0.1 collective-permute-start.12
  82.0 25.3 %collective-permute-done.6.refs_0_.far_q = bf16[8,128,128]{2,1,0:T(8,128)(2,1)S(1)} collective-permute-done((bf16[8,128,128]{2,1,0:T(8,128)(2,1)S(1)}, bf16[8,128,128]{2,1,0:T(8,128)(2,1)S(1)}, u32[]{:S(2)}, u32[]{:S(2)}) %collective-permute-start.6) | collective-permute-done | bytes 262176 | tf_op jit(solution)/shard_map/ppermute | solution.py:349
  107.3 0.0 collective-permute-done.7.refs_1_.far_k
  107.3 0.5 arrived.3.odd_ref
  107.8 0.0 collective-permute-done.10.down_sum
  107.9 0.0 collective-permute-done.12.up_sum
  107.9 1.9 %finish.1 = (bf16[128,2048]{1,0:T(8,128)(2,1)}, bf16[128,2048]{1,0:T(8,128)(2,1)}, bf16[128,2048]{1,0:T(8,128)(2,1)}) custom-call(s32[1]{0:T(128)} %arrived.3.odd_ref, f32[8,128,128]{2,1,0:T(8,128)S(1)} %get-tuple-element.28.q_own, f32[8,256,128]{2,1,0:T(8,128)S(1)} %get-tuple-element.29.kv_a, ...), custom_call_target="tpu_custom_call" | custom-call | flops 1000000 | bytes 6291456 | tf_op jit(solution)/shard_map/finish/pallas_call | solution.py:335
Async XLA Ops:
  1.4 0.7 copy-start
  5.3 30.1 %collective-permute-start.4 = (bf16[8,272,128]{2,1,0:T(8,128)(2,1)S(1)}, bf16[8,272,128]{2,1,0:T(8,128)(2,1)S(1)}, u32[]{:S(2)}, u32[]{:S(2)}) collective-permute-start(bf16[8,272,128]{2,1,0:T(8,128)(2,1)S(1)} %get-tuple-element.24.xqa), channel_id=1, source_target_pairs={{0,2},{1,3},{2,4},{3,5},{4,6},{5,7},{6,8},{7,9},{8,10},{9,11},{10,... | collective-permute-start | bytes 1671176 | tf_op jit(solution)/shard_map/ppermute | solution.py:349
  7.9 48.8 %collective-permute-start.2 = (bf16[8,272,128]{2,1,0:T(8,128)(2,1)S(1)}, bf16[8,272,128]{2,1,0:T(8,128)(2,1)S(1)}, u32[]{:S(2)}, u32[]{:S(2)}) collective-permute-start(bf16[8,272,128]{2,1,0:T(8,128)(2,1)S(1)} %get-tuple-element.22), channel_id=1, source_target_pairs={{0,29},{1,4},{2,31},{3,6},{4,1},{5,8},{6,3},{7,10},{8,5},{9,12},{1... | collective-permute-start | bytes 1671176 | tf_op jit(solution)/shard_map/ppermute | solution.py:359
  11.7 44.9 %collective-permute-start = (bf16[8,272,128]{2,1,0:T(8,128)(2,1)S(1)}, bf16[8,272,128]{2,1,0:T(8,128)(2,1)S(1)}, u32[]{:S(2)}, u32[]{:S(2)}) collective-permute-start(bf16[8,272,128]{2,1,0:T(8,128)(2,1)S(1)} %get-tuple-element.20.xqb), channel_id=1, source_target_pairs={{0,32},{32,64},{64,96},{96,128},{128,160},{160,192},{192,224},{224... | collective-permute-start | bytes 1671176 | tf_op jit(solution)/shard_map/ppermute | solution.py:349
  14.6 20.8 %collective-permute-start.3 = (bf16[8,256,128]{2,1,0:T(8,128)(2,1)S(1)}, bf16[8,256,128]{2,1,0:T(8,128)(2,1)S(1)}, u32[]{:S(2)}, u32[]{:S(2)}) collective-permute-start(bf16[8,256,128]{2,1,0:T(8,128)(2,1)S(1)} %get-tuple-element.23.xkb), channel_id=1, source_target_pairs={{0,30},{1,31},{2,0},{3,1},{4,2},{5,3},{6,4},{7,5},{8,6},{9,7},{10,... | collective-permute-start | bytes 1572872 | tf_op jit(solution)/shard_map/ppermute | solution.py:349
  16.0 40.7 %collective-permute-start.1 = (bf16[8,256,128]{2,1,0:T(8,128)(2,1)S(1)}, bf16[8,256,128]{2,1,0:T(8,128)(2,1)S(1)}, u32[]{:S(2)}, u32[]{:S(2)}) collective-permute-start(bf16[8,256,128]{2,1,0:T(8,128)(2,1)S(1)} %get-tuple-element.21.xka), channel_id=1, source_target_pairs={{0,224},{32,0},{64,32},{96,64},{128,96},{160,128},{192,160},{224,1... | collective-permute-start | bytes 1572872 | tf_op jit(solution)/shard_map/ppermute | solution.py:349
  35.6 21.6 %collective-permute-start.5 = (bf16[8,800,128]{2,1,0:T(8,128)(2,1)S(1)}, bf16[8,800,128]{2,1,0:T(8,128)(2,1)S(1)}, u32[]{:S(2)}, u32[]{:S(2)}) collective-permute-start(bf16[8,800,128]{2,1,0:T(8,128)(2,1)S(1)} %mates.1), channel_id=1, source_target_pairs={{0,1},{1,0},{2,3},{3,2},{4,5},{5,4},{6,7},{7,6},{8,9},{9,8},{10,11... | collective-permute-start | bytes 4915208 | tf_op jit(solution)/shard_map/ppermute | solution.py:354
  67.9 6.7 %collective-permute-start.9 = (bf16[8,384,128]{2,1,0:T(8,128)(2,1)S(1)}, bf16[8,384,128]{2,1,0:T(8,128)(2,1)S(1)}, u32[]{:S(2)}, u32[]{:S(2)}) collective-permute-start(bf16[8,384,128]{2,1,0:T(8,128)(2,1)S(1)} %get-tuple-element.32), channel_id=1, source_target_pairs={{0,1},{1,0},{2,3},{3,2},{4,5},{5,4},{6,7},{7,6},{8,9},{9,8},{10,11... | collective-permute-start | bytes 2359304 | tf_op jit(solution)/shard_map/ppermute | solution.py:354
  68.4 13.2 %collective-permute-start.11 = (bf16[8,256,128]{2,1,0:T(8,128)(2,1)S(1)}, bf16[8,256,128]{2,1,0:T(8,128)(2,1)S(1)}, u32[]{:S(2)}, u32[]{:S(2)}) collective-permute-start(bf16[8,256,128]{2,1,0:T(8,128)(2,1)S(1)} %get-tuple-element.35), channel_id=1, source_target_pairs={{0,1},{1,2},{2,3},{3,4},{4,5},{5,6},{6,7},{7,8},{8,9},{9,10},{10,1... | collective-permute-start | bytes 1572872 | tf_op jit(solution)/shard_map/ppermute | solution.py:349
  68.4 38.9 %collective-permute-start.7 = (bf16[8,256,128]{2,1,0:T(8,128)(2,1)S(1)}, bf16[8,256,128]{2,1,0:T(8,128)(2,1)S(1)}, u32[]{:S(2)}, u32[]{:S(2)}) collective-permute-start(bf16[8,256,128]{2,1,0:T(8,128)(2,1)S(1)} %get-tuple-element.27), channel_id=1, source_target_pairs={{0,32},{32,64},{64,96},{96,128},{128,160},{160,192},{192,224},{224... | collective-permute-start | bytes 1572872 | tf_op jit(solution)/shard_map/ppermute | solution.py:349
  68.5 6.1 %collective-permute-start.8 = (bf16[8,128,128]{2,1,0:T(8,128)(2,1)S(1)}, bf16[8,128,128]{2,1,0:T(8,128)(2,1)S(1)}, u32[]{:S(2)}, u32[]{:S(2)}) collective-permute-start(bf16[8,128,128]{2,1,0:T(8,128)(2,1)S(1)} %get-tuple-element.30), channel_id=1, source_target_pairs={{0,31},{1,0},{2,1},{3,2},{4,3},{5,4},{6,5},{7,6},{8,7},{9,8},{10,9... | collective-permute-start | bytes 786440 | tf_op jit(solution)/shard_map/ppermute | solution.py:349
  69.3 38.0 %collective-permute-start.6 = (bf16[8,128,128]{2,1,0:T(8,128)(2,1)S(1)}, bf16[8,128,128]{2,1,0:T(8,128)(2,1)S(1)}, u32[]{:S(2)}, u32[]{:S(2)}) collective-permute-start(bf16[8,128,128]{2,1,0:T(8,128)(2,1)S(1)} %get-tuple-element.25), channel_id=1, source_target_pairs={{0,224},{32,0},{64,32},{96,64},{128,96},{160,128},{192,160},{224,1... | collective-permute-start | bytes 786440 | tf_op jit(solution)/shard_map/ppermute | solution.py:349
  74.7 33.1 %collective-permute-start.10 = (bf16[8,128,128]{2,1,0:T(8,128)(2,1)S(1)}, bf16[8,128,128]{2,1,0:T(8,128)(2,1)S(1)}, u32[]{:S(2)}, u32[]{:S(2)}) collective-permute-start(bf16[8,128,128]{2,1,0:T(8,128)(2,1)S(1)} %combine_a.1), channel_id=1, source_target_pairs={{0,30},{1,31},{2,0},{3,1},{4,2},{5,3},{6,4},{7,5},{8,6},{9,7},{10,... | collective-permute-start | bytes 786440 | tf_op jit(solution)/shard_map/ppermute | solution.py:349
  81.9 26.0 %collective-permute-start.12 = (bf16[8,256,128]{2,1,0:T(8,128)(2,1)S(1)}, bf16[8,256,128]{2,1,0:T(8,128)(2,1)S(1)}, u32[]{:S(2)}, u32[]{:S(2)}) collective-permute-start(bf16[8,256,128]{2,1,0:T(8,128)(2,1)S(1)} %combine_b.1), channel_id=1, source_target_pairs={{0,2},{1,3},{2,4},{3,5},{4,6},{5,7},{6,8},{7,9},{8,10},{9,11},{10,... | collective-permute-start | bytes 1572872 | tf_op jit(solution)/shard_map/ppermute | solution.py:349
where the time goes:
time: 110 us
  waiting for transfers between devices  53.9 us (49%)
  starting transfers between devices  36.4 us (33%)
  Pallas kernels  17.3 us (16%)
  local copies, waits for them, and re-layouts  1.47 us (1%)
    ppermute x10, waiting for transfers between devices, moved(): lax.ppermute(value, axis, [(i, (i + steps) % count) for i in range(count)])  53.9 us
    ppermute x10, starting transfers between devices, moved(): lax.ppermute(value, axis, [(i, (i + steps) % count) for i in range(count)])  23.1 us
    pallas_call x5, Pallas kernels, call_on_chip(): pl.pallas_call(kernel, in_specs=[pl.BlockSpec(memory_space=pltpu.SMEM)] +...  11.1 us
    ppermute x2, starting transfers between devices, exchanged(): return lax.ppermute(value, 'ka', [(i, i ^ 1) for i in range(count)])  9.49 us
    ppermute x1, starting transfers between devices, crossed(): lax.ppermute(value, 'ka', [(i, (i + (3 if i % 2 == 1 else -3)) % count) f...  3.86 us
    pallas_call x1, Pallas kernels, pack(): pl.pallas_call(pack_kernel, in_specs=[smem, smem, spec] + [anywhere] * 5,...  3.2 us
  transfers between devices with their start and end apart: 13, of which 4 were waited for; matrix products, arithmetic and copies ran while one was open for 0% of the time, Pallas kernels for 1%

commit v1 on v0

--- a/solution.py
+++ b/solution.py
@@ -40,7 +40,7 @@
     for i, row in enumerate(rows):
         stat = jnp.where(line == i, jnp.broadcast_to(row, (STAT, BLOCK)), stat)
     for i in range(2 * WINDOW):
-        flag = (adj_ref[0, i // WINDOW, i % WINDOW, 0] == 1).astype(jnp.int32).astype(F32)
+        flag = (adj_ref[0, i // WINDOW, 0, i % WINDOW] == 1).astype(jnp.int32).astype(F32)
         stat = jnp.where(line == 8 + i, flag, stat)
     return stat.astype(BF16)
 
@@ -121,8 +121,10 @@
 PACK_STEP = 4
 
 
-def pack_kernel(odd_ref, adj_ref, lse_ref, q_hbm, k_hbm, v_hbm, o_hbm, g_hbm,
-                xqa, xka, xqb, xkb, cross, q_in, k_in, v_in, o_in, g_in, sems):
+def pack_kernel(odd_ref, adj_ref, lse_hbm, q_hbm, k_hbm, v_hbm, o_hbm, g_hbm,
+                xqa, xka, xqb, xkb, cross, q_in, k_in, v_in, o_in, g_in, lse_ref, sems, lse_sem):
+    lse_copy = pltpu.make_async_copy(lse_hbm, lse_ref, lse_sem)
+    lse_copy.start()
     width = PACK_STEP * HEAD_DIM
     chunks = 2 * HALF // PACK_STEP
     copies = []
@@ -134,6 +136,7 @@
                 [(q_hbm, q_in), (g_hbm, g_in), (o_hbm, o_in), (k_hbm, k_in), (v_hbm, v_in)])])
         for copy in copies[c]:
             copy.start()
+    lse_copy.wait()
     for c in range(chunks):
         for copy in copies[c]:
             copy.wait()
@@ -166,16 +169,17 @@
     shapes = [QROWS, KROWS, QROWS, KROWS, QROWS]
     return pl.pallas_call(
         pack_kernel,
-        in_specs=[smem, smem, spec] + [anywhere] * 5,
+        in_specs=[smem, smem] + [anywhere] * 6,
         out_specs=[spec] * len(shapes),
         out_shape=[vmem((HALF, s, HEAD_DIM), BF16) for s in shapes],
         scratch_shapes=[pltpu.VMEM((BLOCK, 2 * HALF * HEAD_DIM), BF16)] * 5
-        + [pltpu.SemaphoreType.DMA((2 * HALF // PACK_STEP, 5))],
+        + [pltpu.VMEM((2 * HALF, BLOCK), F32), pltpu.SemaphoreType.DMA((2 * HALF // PACK_STEP, 5)),
+           pltpu.SemaphoreType.DMA],
         compiler_params=pltpu.CompilerParams(vmem_limit_bytes=16 * 2**20),
         cost_estimate=pl.CostEstimate(flops=10**8, bytes_accessed=5 * 2**20, transcendentals=0),
         name="pack",
-    )(odd, adjacency, row_lse, *[pltpu.with_memory_space_constraint(x, pltpu.HBM)
-                                 for x in (queries, keys, values, outputs, d_out)])
+    )(odd, adjacency, *[pltpu.with_memory_space_constraint(x, pltpu.HBM)
+                        for x in (row_lse, queries, keys, values, outputs, d_out)])
 
 
 Q3 = slice(0, QROWS)
@@ -204,7 +208,7 @@
         out[:, NEAR_Q, :] = xqa[...]
 
 
-def attend_a_kernel(odd_ref, xqa, cross, q2, mates, xka, fk, swap_b,
+def attend_a_kernel(odd_ref, xqa, cross, q2, mates, xka, fk,
                     q_own, q_two, kv_own, swap_out, down_out, far_out):
     odd = odd_ref[0]
     is_odd = odd == 1
@@ -225,8 +229,7 @@
         q_own[h] = dq[0:128]
         down_out[h] = dq[128:256].astype(BF16)
         q_two[h] = dq[256:384]
-        swap_out[h, 0:128] = dq[384:512].astype(BF16)
-        swap_out[h, 128:384] = swap_b[h]
+        swap_out[h] = dq[384:512].astype(BF16)
         kv_own[h, 0:128] = dk[0:128]
         kv_own[h, 128:256] = dv[0:128]
         far_out[h, 0:128] = dk[128:256].astype(BF16)
@@ -276,7 +279,7 @@
 
 
 def attend_a(odd, *inputs):
-    outs = [block(128, F32), block(128, F32), block(256, F32), block(384, BF16), block(128, BF16), block(256, BF16)]
+    outs = [block(128, F32), block(128, F32), block(256, F32), block(128, BF16), block(128, BF16), block(256, BF16)]
     return call_on_chip(attend_a_kernel, "attend_a", odd, inputs, outs, 13 * 10**8, 2**20)
 
 
@@ -285,37 +288,30 @@
     return call_on_chip(attend_b_kernel, "attend_b", odd, inputs, outs, 13 * 10**8, 2**20)
 
 
-def combine_kernel(parity, rows, odd_ref, mine, swapped, relayed_in, total):
-    taken = odd_ref[0] == parity
-
+def combine_kernel(odd_ref, mine, swapped, total):
     def one_head(h, carry):
-        relay = jnp.where(taken, relayed_in[h].astype(F32), 0.0)
-        total[h] = (mine[h] + swapped[h, rows].astype(F32) + relay).astype(BF16)
+        total[h] = (mine[h] + swapped[h].astype(F32)).astype(BF16)
         return carry
 
     lax.fori_loop(0, HALF, one_head, 0)
 
 
-def combine(parity, rows, name, odd, *inputs):
-    return call_on_chip(functools.partial(combine_kernel, parity, rows), name, odd, inputs,
-                        [(inputs[0].shape, BF16)], 10**6)[0]
+def combine(name, odd, *inputs):
+    return call_on_chip(combine_kernel, name, odd, inputs, [(inputs[0].shape, BF16)], 10**6)[0]
 
 
 def finish_kernel(odd_ref, q_own, kv_a, down, down_sum, far_k, k_own, q_b, up, up_sum, far_q,
                   dq_hbm, dk_hbm, dv_hbm, dq, dk, dv, sems):
-    odd = odd_ref[0]
     copies = []
     for head in range(2 * HALF):
         h = head % HALF
         cols = slice(head * HEAD_DIM, (head + 1) * HEAD_DIM)
         if head < HALF:
-            from_down = jnp.where(odd == 1, 0.0, down[h].astype(F32))
-            grad_q = q_own[h] + down_sum[h].astype(F32) + from_down
+            grad_q = q_own[h] + down_sum[h].astype(F32) + down[h].astype(F32)
             grad_kv = kv_a[h] + far_k[h].astype(F32)
         else:
-            from_up = jnp.where(odd == 1, up[h].astype(F32), 0.0)
             grad_q = q_b[h] + far_q[h].astype(F32)
-            grad_kv = k_own[h] + up_sum[h].astype(F32) + from_up
+            grad_kv = k_own[h] + up_sum[h].astype(F32) + up[h].astype(F32)
         dq[:, cols] = grad_q.astype(BF16)
         dk[:, cols] = grad_kv[0:128].astype(BF16)
         dv[:, cols] = grad_kv[128:256].astype(BF16)
@@ -354,31 +350,38 @@
     return lax.ppermute(value, "ka", [(i, i ^ 1) for i in range(count)])
 
 
-def crossed(value):
+def crossed(value, odd_steps, even_steps):
     count = lax.axis_size("ka")
-    return lax.ppermute(value, "ka", [(i, (i + (3 if i % 2 == 1 else -3)) % count) for i in range(count)])
+    return lax.ppermute(
+        value, "ka", [(i, (i + (odd_steps if i % 2 == 1 else even_steps)) % count) for i in range(count)])
 
 
 def local(queries, keys, values, outputs, d_out, row_lse, adjacency):
     odd = (lax.axis_index("ka") % 2).astype(jnp.int32).reshape(1)
-    xqa, xka, xqb, xkb, cross = pack(odd, adjacency, queries, keys, values, outputs, d_out, row_lse)
+    xqa, xka, xqb, xkb, cross = pack(
+        odd, adjacency.transpose(0, 1, 3, 2), queries, keys, values, outputs, d_out, row_lse)
+    fq = moved(xqb, "pb", 1)
     q2 = moved(xqa, "ka", 2)
     k2 = moved(xkb, "ka", -2)
-    fq = moved(xqb, "pb", 1)
+    cross = crossed(cross, 3, -3)
+    mates = call_on_chip(mates_kernel, "mates", odd, (xqa, xkb, q2, k2), [block(MATE_ROWS, BF16)], 10**5)[0]
+    mates, xka = lax.optimization_barrier((mates, xka))
+    mates = exchanged(mates)
     fk = moved(xka, "pb", -1)
-    cross = crossed(cross)
-    mates = exchanged(call_on_chip(mates_kernel, "mates", odd, (xqa, xkb, q2, k2), [block(MATE_ROWS, BF16)], 10**5)[0])
-    here = arrived(odd, fq, fk, cross)
+    here = arrived(odd, fq, cross)
     k_own, k_two, q_b, swap_b, up, far_q = attend_b(here, xkb, cross, k2, mates, xqb, fq)
-    up = moved(up, "ka", 1)
+    up = crossed(up, 3, 1)
     far_q = moved(far_q, "pb", -1)
-    q_own, q_two, kv_a, swap, down, far_k = attend_a(here, xqa, cross, q2, mates, xka, fk, swap_b)
-    down = moved(down, "ka", -1)
-    swap = exchanged(swap)
+    swap_b, fk = lax.optimization_barrier((exchanged(swap_b), fk))
+    b_sum = combine("combine_b", odd, k_two, swap_b)
+    xka, b_sum = lax.optimization_barrier((xka, b_sum))
+    up_sum = moved(b_sum, "ka", 2)
+    q_own, q_two, kv_a, swap_a, down, far_k = attend_a(here, xqa, cross, q2, mates, xka, fk)
+    down, swap_a, far_k, far_q = lax.optimization_barrier((down, swap_a, far_k, far_q))
+    down = crossed(down, -1, -3)
     far_k = moved(far_k, "pb", 1)
-    up_sum = moved(combine(0, slice(128, 384), "combine_b", odd, k_two, swap, up), "ka", 2)
-    down_sum = moved(combine(1, slice(0, 128), "combine_a", odd, q_two, swap, down), "ka", -2)
-    here = arrived(odd, far_q, far_k)
+    down_sum = moved(combine("combine_a", odd, q_two, exchanged(swap_a)), "ka", -2)
+    here = arrived(odd, far_q, up, up_sum)
     return tuple(finish(here, q_own, kv_a, down, down_sum, far_k, k_own, q_b, up, up_sum, far_q))
 
 

time: 110 us -> 96.6 us (0.88)
  waiting for transfers between devices: 53.9 us -> 41.7 us
    ppermute x10 -> x8, waiting for transfers between devices: 53.9 us -> 41.7 us  [moved(): lax.ppermute(value, axis, [(i, (i + steps) % count) for i in range(count)])]
    ppermute x2 -> x3, starting transfers between devices: 9.49 us -> 7.6 us  [exchanged(): return lax.ppermute(value, 'ka', [(i, i ^ 1) for i in range(count)])]
    ppermute x10 -> x8, starting transfers between devices: 23.1 us -> 23.9 us  [moved(): lax.ppermute(value, axis, [(i, (i + steps) % count) for i in range(count)])]
    ppermute x1 -> x3, starting transfers between devices: 3.86 us -> 4.42 us  [crossed(): lax.ppermute(value, 'ka', [(i, (i + (odd_steps if i % 2 == 1 else even_st...]
  transfers between devices with their start and end apart: 13 -> 14, of which waited for: 4 -> 6; matrix products, arithmetic and copies ran while one was open for 0% -> 0% of each run, Pallas kernels for 1% -> 12%
where the time goes in v1:
time: 96.6 us; the launch traced here: 96.4 us
  waiting for transfers between devices  41.7 us (43%)
  starting transfers between devices  35.9 us (37%)
  Pallas kernels  17.4 us (18%)
    ppermute x8, waiting for transfers between devices, moved(): lax.ppermute(value, axis, [(i, (i + steps) % count) for i in range(count)])  41.7 us
    ppermute x8, starting transfers between devices, moved(): lax.ppermute(value, axis, [(i, (i + steps) % count) for i in range(count)])  23.9 us
    pallas_call x5, Pallas kernels, call_on_chip(): pl.pallas_call(kernel, in_specs=[pl.BlockSpec(memory_space=pltpu.SMEM)] +...  11 us
    ppermute x3, starting transfers between devices, exchanged(): return lax.ppermute(value, 'ka', [(i, i ^ 1) for i in range(count)])  7.6 us
    ppermute x3, starting transfers between devices, crossed(): lax.ppermute(value, 'ka', [(i, (i + (odd_steps if i % 2 == 1 else even_st...  4.42 us
    pallas_call x1, Pallas kernels, pack(): pl.pallas_call(pack_kernel, in_specs=[smem, smem] + [anywhere] * 6, out_s...  3.56 us
  transfers between devices with their start and end apart: 14, of which 6 were waited for; matrix products, arithmetic and copies ran while one was open for 0% of the time, Pallas kernels for 12%

profile of v1, /device:TPU:1, one launch (start us, length us, event | category | flops | bytes accessed | tf_op | source)
XLA Modules:
  0.0 96.4 jit_solution(14726063124676517665)
XLA Ops:
  0.6 0.0 copy-start
  0.7 0.7 copy-done
  1.3 3.6 %pack.1 = (bf16[8,272,128]{2,1,0:T(8,128)(2,1)S(1)}, bf16[8,256,128]{2,1,0:T(8,128)(2,1)S(1)}, bf16[8,272,128]{2,1,0:T(8,128)(2,1)S(1)}, bf16[8,256,128]{2,1,0:T(8,128)(2,1)S(1)}, bf16[8,272,128]{2,1,0:T(8,128)(2,1)S(1)}) custom-call(s32[1]{0:T(128)} %bitcast.odd_ref, s32[1,2,1,4]{3,2,1,0:T(1,128)S(1)} %bitcast.4, f32[16,128]{1,0:T(8,128)} %lse_hbm.1, ...), custom_call_target="tpu_custom_call" | custom-call | flops 100000000 | bytes 5242880 | tf_op jit(solution)/shard_map/pack/pallas_call | solution.py:170
  4.9 2.5 %collective-permute-start.2 = (bf16[8,272,128]{2,1,0:T(8,128)(2,1)S(1)}, bf16[8,272,128]{2,1,0:T(8,128)(2,1)S(1)}, u32[]{:S(2)}, u32[]{:S(2)}) collective-permute-start(bf16[8,272,128]{2,1,0:T(8,128)(2,1)S(1)} %get-tuple-element.32.xqa), channel_id=1, source_target_pairs={{0,2},{1,3},{2,4},{3,5},{4,6},{5,7},{6,8},{7,9},{8,10},{9,11},{10,... | collective-permute-start | bytes 1671176 | tf_op jit(solution)/shard_map/ppermute | solution.py:345
  7.4 2.9 %collective-permute-start = (bf16[8,272,128]{2,1,0:T(8,128)(2,1)S(1)}, bf16[8,272,128]{2,1,0:T(8,128)(2,1)S(1)}, u32[]{:S(2)}, u32[]{:S(2)}) collective-permute-start(bf16[8,272,128]{2,1,0:T(8,128)(2,1)S(1)} %get-tuple-element.30.xqb), channel_id=1, source_target_pairs={{0,32},{32,64},{64,96},{96,128},{128,160},{160,192},{192,224},{224... | collective-permute-start | bytes 1671176 | tf_op jit(solution)/shard_map/ppermute | solution.py:345
  10.3 4.1 %collective-permute-start.1 = (bf16[8,272,128]{2,1,0:T(8,128)(2,1)S(1)}, bf16[8,272,128]{2,1,0:T(8,128)(2,1)S(1)}, u32[]{:S(2)}, u32[]{:S(2)}) collective-permute-start(bf16[8,272,128]{2,1,0:T(8,128)(2,1)S(1)} %get-tuple-element.31), channel_id=1, source_target_pairs={{0,29},{1,4},{2,31},{3,6},{4,1},{5,8},{6,3},{7,10},{8,5},{9,12},{1... | collective-permute-start | bytes 1671176 | tf_op jit(solution)/shard_map/ppermute | solution.py:355
  14.5 1.9 %collective-permute-start.3 = (bf16[8,256,128]{2,1,0:T(8,128)(2,1)S(1)}, bf16[8,256,128]{2,1,0:T(8,128)(2,1)S(1)}, u32[]{:S(2)}, u32[]{:S(2)}) collective-permute-start(bf16[8,256,128]{2,1,0:T(8,128)(2,1)S(1)} %get-tuple-element.33.xkb), channel_id=1, source_target_pairs={{0,30},{1,31},{2,0},{3,1},{4,2},{5,3},{6,4},{7,5},{8,6},{9,7},{10,... | collective-permute-start | bytes 1572872 | tf_op jit(solution)/shard_map/ppermute | solution.py:345
  16.4 17.7 %collective-permute-done.3.k2 = bf16[8,256,128]{2,1,0:T(8,128)(2,1)S(1)} collective-permute-done((bf16[8,256,128]{2,1,0:T(8,128)(2,1)S(1)}, bf16[8,256,128]{2,1,0:T(8,128)(2,1)S(1)}, u32[]{:S(2)}, u32[]{:S(2)}) %collective-permute-start.3) | collective-permute-done | bytes 524320 | tf_op jit(solution)/shard_map/ppermute | solution.py:345
  34.1 0.0 collective-permute-done.2.q2
  34.1 0.1 mates.1
  34.2 6.2 %collective-permute-start.4 = (bf16[8,800,128]{2,1,0:T(8,128)(2,1)S(1)}, bf16[8,800,128]{2,1,0:T(8,128)(2,1)S(1)}, u32[]{:S(2)}, u32[]{:S(2)}) collective-permute-start(bf16[8,800,128]{2,1,0:T(8,128)(2,1)S(1)} %mates.1), channel_id=1, source_target_pairs={{0,1},{1,0},{2,3},{3,2},{4,5},{5,4},{6,7},{7,6},{8,9},{9,8},{10,11... | collective-permute-start | bytes 4915208 | tf_op jit(solution)/shard_map/ppermute | solution.py:350
  40.4 7.1 %collective-permute-start.6 = (bf16[8,256,128]{2,1,0:T(8,128)(2,1)S(1)}, bf16[8,256,128]{2,1,0:T(8,128)(2,1)S(1)}, u32[]{:S(2)}, u32[]{:S(2)}) collective-permute-start(bf16[8,256,128]{2,1,0:T(8,128)(2,1)S(1)} %get-tuple-element.40.xka), channel_id=1, source_target_pairs={{0,224},{32,0},{64,32},{96,64},{128,96},{160,128},{192,160},{224,1... | collective-permute-start | bytes 1572872 | tf_op jit(solution)/shard_map/ppermute | solution.py:345
  47.6 0.0 collective-permute-done.refs_0_.fq
  47.6 0.0 collective-permute-done.1.refs_1_.cross
  47.6 0.5 arrived.2.odd_ref
  48.1 0.0 collective-permute-done.4.mates
  48.1 5.2 %attend_b.1 = (f32[8,256,128]{2,1,0:T(8,128)S(1)}, f32[8,256,128]{2,1,0:T(8,128)S(1)}, f32[8,128,128]{2,1,0:T(8,128)S(1)}, bf16[8,256,128]{2,1,0:T(8,128)(2,1)S(...) custom-call(s32[1]{0:T(128)} %arrived.2.odd_ref, bf16[8,256,128]{2,1,0:T(8,128)(2,1)S(1)} %get-tuple-element.33.xkb, ...), custom_call_target="tpu_custom_call" | custom-call | flops 1300000000 | bytes 4358144 | tf_op jit(solution)/shard_map/attend_b/pallas_call | solution.py:91
  53.3 0.4 collective-permute-start.5
  53.7 2.6 %collective-permute-start.7 = (bf16[8,128,128]{2,1,0:T(8,128)(2,1)S(1)}, bf16[8,128,128]{2,1,0:T(8,128)(2,1)S(1)}, u32[]{:S(2)}, u32[]{:S(2)}) collective-permute-start(bf16[8,128,128]{2,1,0:T(8,128)(2,1)S(1)} %get-tuple-element.45), channel_id=1, source_target_pairs={{0,224},{32,0},{64,32},{96,64},{128,96},{160,128},{192,160},{224,1... | collective-permute-start | bytes 786440 | tf_op jit(solution)/shard_map/ppermute | solution.py:345
  56.3 0.0 collective-permute-start.8
  56.3 2.8 %collective-permute-done.6.fk = bf16[8,256,128]{2,1,0:T(8,128)(2,1)S(1)} collective-permute-done((bf16[8,256,128]{2,1,0:T(8,128)(2,1)S(1)}, bf16[8,256,128]{2,1,0:T(8,128)(2,1)S(1)}, u32[]{:S(2)}, u32[]{:S(2)}) %collective-permute-start.6) | collective-permute-done | bytes 524320 | tf_op jit(solution)/shard_map/ppermute | solution.py:345
  59.1 0.0 collective-permute-done.5.swapped
  59.1 0.1 combine_b.1
  59.2 2.0 %collective-permute-start.9 = (bf16[8,256,128]{2,1,0:T(8,128)(2,1)S(1)}, bf16[8,256,128]{2,1,0:T(8,128)(2,1)S(1)}, u32[]{:S(2)}, u32[]{:S(2)}) collective-permute-start(bf16[8,256,128]{2,1,0:T(8,128)(2,1)S(1)} %combine_b.1), channel_id=1, source_target_pairs={{0,2},{1,3},{2,4},{3,5},{4,6},{5,7},{6,8},{7,9},{8,10},{9,11},{10,... | collective-permute-start | bytes 1572872 | tf_op jit(solution)/shard_map/ppermute | solution.py:345
  61.3 5.5 %attend_a.1 = (f32[8,128,128]{2,1,0:T(8,128)S(1)}, f32[8,128,128]{2,1,0:T(8,128)S(1)}, f32[8,256,128]{2,1,0:T(8,128)S(1)}, bf16[8,128,128]{2,1,0:T(8,128)(2,1)S(...) custom-call(s32[1]{0:T(128)} %arrived.2.odd_ref, bf16[8,272,128]{2,1,0:T(8,128)(2,1)S(1)} %get-tuple-element.32.xqa, ...), custom_call_target="tpu_custom_call" | custom-call | flops 1300000000 | bytes 4358144 | tf_op jit(solution)/shard_map/attend_a/pallas_call | solution.py:91
  66.7 5.0 %collective-permute-done.7.refs_0_.far_q = bf16[8,128,128]{2,1,0:T(8,128)(2,1)S(1)} collective-permute-done((bf16[8,128,128]{2,1,0:T(8,128)(2,1)S(1)}, bf16[8,128,128]{2,1,0:T(8,128)(2,1)S(1)}, u32[]{:S(2)}, u32[]{:S(2)}) %collective-permute-start.7) | collective-permute-done | bytes 262176 | tf_op jit(solution)/shard_map/ppermute | solution.py:345
  71.7 0.9 collective-permute-start.11
  72.7 4.7 %collective-permute-start.13 = (bf16[8,256,128]{2,1,0:T(8,128)(2,1)S(1)}, bf16[8,256,128]{2,1,0:T(8,128)(2,1)S(1)}, u32[]{:S(2)}, u32[]{:S(2)}) collective-permute-start(bf16[8,256,128]{2,1,0:T(8,128)(2,1)S(1)} %get-tuple-element.54), channel_id=1, source_target_pairs={{0,32},{32,64},{64,96},{96,128},{128,160},{160,192},{192,224},{224... | collective-permute-start | bytes 1572872 | tf_op jit(solution)/shard_map/ppermute | solution.py:345
  77.4 0.3 collective-permute-start.10
  77.7 0.0 collective-permute-done.11.swapped
  77.7 0.1 combine_a.1
  77.7 0.1 collective-permute-start.12
  77.8 0.0 collective-permute-done.8.refs_1_.up
  77.8 7.9 %collective-permute-done.9.refs_2_.up_sum = bf16[8,256,128]{2,1,0:T(8,128)(2,1)S(1)} collective-permute-done((bf16[8,256,128]{2,1,0:T(8,128)(2,1)S(1)}, bf16[8,256,128]{2,1,0:T(8,128)(2,1)S(1)}, u32[]{:S(2)}, u32[]{:S(2)}) %collective-permute-start.9) | collective-permute-done | bytes 524320 | tf_op jit(solution)/shard_map/ppermute | solution.py:345
  85.8 0.5 arrived.3.odd_ref
  86.3 0.0 collective-permute-done.10.down
  86.3 2.2 %collective-permute-done.12.down_sum = bf16[8,128,128]{2,1,0:T(8,128)(2,1)S(1)} collective-permute-done((bf16[8,128,128]{2,1,0:T(8,128)(2,1)S(1)}, bf16[8,128,128]{2,1,0:T(8,128)(2,1)S(1)}, u32[]{:S(2)}, u32[]{:S(2)}) %collective-permute-start.12) | collective-permute-done | bytes 262176 | tf_op jit(solution)/shard_map/ppermute | solution.py:345
  88.6 6.1 %collective-permute-done.13.far_k = bf16[8,256,128]{2,1,0:T(8,128)(2,1)S(1)} collective-permute-done((bf16[8,256,128]{2,1,0:T(8,128)(2,1)S(1)}, bf16[8,256,128]{2,1,0:T(8,128)(2,1)S(1)}, u32[]{:S(2)}, u32[]{:S(2)}) %collective-permute-start.13) | collective-permute-done | bytes 524320 | tf_op jit(solution)/shard_map/ppermute | solution.py:345
  94.6 1.8 %finish.1 = (bf16[128,2048]{1,0:T(8,128)(2,1)}, bf16[128,2048]{1,0:T(8,128)(2,1)}, bf16[128,2048]{1,0:T(8,128)(2,1)}) custom-call(s32[1]{0:T(128)} %arrived.3.odd_ref, f32[8,128,128]{2,1,0:T(8,128)S(1)} %get-tuple-element.49.q_own, f32[8,256,128]{2,1,0:T(8,128)S(1)} %get-tuple-element.50.kv_a, bf16[8,128,128]{2,1,0:T(8,128)(2,1)S(1)} %collective-permute-done.10.down, ...), custom_call_target="tpu_custom_call" | custom-call | flops 1000000 | bytes 6291456 | tf_op jit(solution)/shard_map/finish/pallas_call | solution.py:331
Async XLA Ops:
  0.6 0.7 copy-start
  4.9 29.2 %collective-permute-start.2 = (bf16[8,272,128]{2,1,0:T(8,128)(2,1)S(1)}, bf16[8,272,128]{2,1,0:T(8,128)(2,1)S(1)}, u32[]{:S(2)}, u32[]{:S(2)}) collective-permute-start(bf16[8,272,128]{2,1,0:T(8,128)(2,1)S(1)} %get-tuple-element.32.xqa), channel_id=1, source_target_pairs={{0,2},{1,3},{2,4},{3,5},{4,6},{5,7},{6,8},{7,9},{8,10},{9,11},{10,... | collective-permute-start | bytes 1671176 | tf_op jit(solution)/shard_map/ppermute | solution.py:345
  7.4 40.1 %collective-permute-start = (bf16[8,272,128]{2,1,0:T(8,128)(2,1)S(1)}, bf16[8,272,128]{2,1,0:T(8,128)(2,1)S(1)}, u32[]{:S(2)}, u32[]{:S(2)}) collective-permute-start(bf16[8,272,128]{2,1,0:T(8,128)(2,1)S(1)} %get-tuple-element.30.xqb), channel_id=1, source_target_pairs={{0,32},{32,64},{64,96},{96,128},{128,160},{160,192},{192,224},{224... | collective-permute-start | bytes 1671176 | tf_op jit(solution)/shard_map/ppermute | solution.py:345
  10.3 37.2 %collective-permute-start.1 = (bf16[8,272,128]{2,1,0:T(8,128)(2,1)S(1)}, bf16[8,272,128]{2,1,0:T(8,128)(2,1)S(1)}, u32[]{:S(2)}, u32[]{:S(2)}) collective-permute-start(bf16[8,272,128]{2,1,0:T(8,128)(2,1)S(1)} %get-tuple-element.31), channel_id=1, source_target_pairs={{0,29},{1,4},{2,31},{3,6},{4,1},{5,8},{6,3},{7,10},{8,5},{9,12},{1... | collective-permute-start | bytes 1671176 | tf_op jit(solution)/shard_map/ppermute | solution.py:355
  14.5 19.6 %collective-permute-start.3 = (bf16[8,256,128]{2,1,0:T(8,128)(2,1)S(1)}, bf16[8,256,128]{2,1,0:T(8,128)(2,1)S(1)}, u32[]{:S(2)}, u32[]{:S(2)}) collective-permute-start(bf16[8,256,128]{2,1,0:T(8,128)(2,1)S(1)} %get-tuple-element.33.xkb), channel_id=1, source_target_pairs={{0,30},{1,31},{2,0},{3,1},{4,2},{5,3},{6,4},{7,5},{8,6},{9,7},{10,... | collective-permute-start | bytes 1572872 | tf_op jit(solution)/shard_map/ppermute | solution.py:345
  34.2 13.9 %collective-permute-start.4 = (bf16[8,800,128]{2,1,0:T(8,128)(2,1)S(1)}, bf16[8,800,128]{2,1,0:T(8,128)(2,1)S(1)}, u32[]{:S(2)}, u32[]{:S(2)}) collective-permute-start(bf16[8,800,128]{2,1,0:T(8,128)(2,1)S(1)} %mates.1), channel_id=1, source_target_pairs={{0,1},{1,0},{2,3},{3,2},{4,5},{5,4},{6,7},{7,6},{8,9},{9,8},{10,11... | collective-permute-start | bytes 4915208 | tf_op jit(solution)/shard_map/ppermute | solution.py:350
  40.4 18.7 %collective-permute-start.6 = (bf16[8,256,128]{2,1,0:T(8,128)(2,1)S(1)}, bf16[8,256,128]{2,1,0:T(8,128)(2,1)S(1)}, u32[]{:S(2)}, u32[]{:S(2)}) collective-permute-start(bf16[8,256,128]{2,1,0:T(8,128)(2,1)S(1)} %get-tuple-element.40.xka), channel_id=1, source_target_pairs={{0,224},{32,0},{64,32},{96,64},{128,96},{160,128},{192,160},{224,1... | collective-permute-start | bytes 1572872 | tf_op jit(solution)/shard_map/ppermute | solution.py:345
  53.3 5.8 %collective-permute-start.5 = (bf16[8,256,128]{2,1,0:T(8,128)(2,1)S(1)}, bf16[8,256,128]{2,1,0:T(8,128)(2,1)S(1)}, u32[]{:S(2)}, u32[]{:S(2)}) collective-permute-start(bf16[8,256,128]{2,1,0:T(8,128)(2,1)S(1)} %get-tuple-element.38), channel_id=1, source_target_pairs={{0,1},{1,0},{2,3},{3,2},{4,5},{5,4},{6,7},{7,6},{8,9},{9,8},{10,11... | collective-permute-start | bytes 1572872 | tf_op jit(solution)/shard_map/ppermute | solution.py:350
  53.7 18.0 %collective-permute-start.7 = (bf16[8,128,128]{2,1,0:T(8,128)(2,1)S(1)}, bf16[8,128,128]{2,1,0:T(8,128)(2,1)S(1)}, u32[]{:S(2)}, u32[]{:S(2)}) collective-permute-start(bf16[8,128,128]{2,1,0:T(8,128)(2,1)S(1)} %get-tuple-element.45), channel_id=1, source_target_pairs={{0,224},{32,0},{64,32},{96,64},{128,96},{160,128},{192,160},{224,1... | collective-permute-start | bytes 786440 | tf_op jit(solution)/shard_map/ppermute | solution.py:345
  56.3 21.5 %collective-permute-start.8 = (bf16[8,256,128]{2,1,0:T(8,128)(2,1)S(1)}, bf16[8,256,128]{2,1,0:T(8,128)(2,1)S(1)}, u32[]{:S(2)}, u32[]{:S(2)}) collective-permute-start(bf16[8,256,128]{2,1,0:T(8,128)(2,1)S(1)} %get-tuple-element.47), channel_id=1, source_target_pairs={{0,1},{1,4},{2,3},{3,6},{4,5},{5,8},{6,7},{7,10},{8,9},{9,12},{10,... | collective-permute-start | bytes 1572872 | tf_op jit(solution)/shard_map/ppermute | solution.py:355
  59.2 26.5 %collective-permute-start.9 = (bf16[8,256,128]{2,1,0:T(8,128)(2,1)S(1)}, bf16[8,256,128]{2,1,0:T(8,128)(2,1)S(1)}, u32[]{:S(2)}, u32[]{:S(2)}) collective-permute-start(bf16[8,256,128]{2,1,0:T(8,128)(2,1)S(1)} %combine_b.1), channel_id=1, source_target_pairs={{0,2},{1,3},{2,4},{3,5},{4,6},{5,7},{6,8},{7,9},{8,10},{9,11},{10,... | collective-permute-start | bytes 1572872 | tf_op jit(solution)/shard_map/ppermute | solution.py:345
  71.7 5.9 %collective-permute-start.11 = (bf16[8,128,128]{2,1,0:T(8,128)(2,1)S(1)}, bf16[8,128,128]{2,1,0:T(8,128)(2,1)S(1)}, u32[]{:S(2)}, u32[]{:S(2)}) collective-permute-start(bf16[8,128,128]{2,1,0:T(8,128)(2,1)S(1)} %get-tuple-element.53), channel_id=1, source_target_pairs={{0,1},{1,0},{2,3},{3,2},{4,5},{5,4},{6,7},{7,6},{8,9},{9,8},{10,11... | collective-permute-start | bytes 786440 | tf_op jit(solution)/shard_map/ppermute | solution.py:350
  72.7 22.0 %collective-permute-start.13 = (bf16[8,256,128]{2,1,0:T(8,128)(2,1)S(1)}, bf16[8,256,128]{2,1,0:T(8,128)(2,1)S(1)}, u32[]{:S(2)}, u32[]{:S(2)}) collective-permute-start(bf16[8,256,128]{2,1,0:T(8,128)(2,1)S(1)} %get-tuple-element.54), channel_id=1, source_target_pairs={{0,32},{32,64},{64,96},{96,128},{128,160},{160,192},{192,224},{224... | collective-permute-start | bytes 1572872 | tf_op jit(solution)/shard_map/ppermute | solution.py:345
  77.4 8.9 %collective-permute-start.10 = (bf16[8,128,128]{2,1,0:T(8,128)(2,1)S(1)}, bf16[8,128,128]{2,1,0:T(8,128)(2,1)S(1)}, u32[]{:S(2)}, u32[]{:S(2)}) collective-permute-start(bf16[8,128,128]{2,1,0:T(8,128)(2,1)S(1)} %get-tuple-element.51), channel_id=1, source_target_pairs={{0,29},{1,0},{2,31},{3,2},{4,1},{5,4},{6,3},{7,6},{8,5},{9,8},{10,... | collective-permute-start | bytes 786440 | tf_op jit(solution)/shard_map/ppermute | solution.py:355
  77.7 10.8 %collective-permute-start.12 = (bf16[8,128,128]{2,1,0:T(8,128)(2,1)S(1)}, bf16[8,128,128]{2,1,0:T(8,128)(2,1)S(1)}, u32[]{:S(2)}, u32[]{:S(2)}) collective-permute-start(bf16[8,128,128]{2,1,0:T(8,128)(2,1)S(1)} %combine_a.1), channel_id=1, source_target_pairs={{0,30},{1,31},{2,0},{3,1},{4,2},{5,3},{6,4},{7,5},{8,6},{9,7},{10,... | collective-permute-start | bytes 786440 | tf_op jit(solution)/shard_map/ppermute | solution.py:345

commit v2 on v1

--- a/solution.py
+++ b/solution.py
@@ -121,8 +121,10 @@
 PACK_STEP = 4
 
 
-def pack_kernel(odd_ref, adj_ref, lse_hbm, q_hbm, k_hbm, v_hbm, o_hbm, g_hbm,
-                xqa, xka, xqb, xkb, cross, q_in, k_in, v_in, o_in, g_in, lse_ref, sems, lse_sem):
+def pack_kernel(odd_ref, adj_hbm, lse_hbm, q_hbm, k_hbm, v_hbm, o_hbm, g_hbm,
+                xqa, xka, xqb, xkb, cross, q_in, k_in, v_in, o_in, g_in, lse_ref, adj_ref, sems, lse_sem, adj_sem):
+    adj_copy = pltpu.make_async_copy(adj_hbm, adj_ref, adj_sem)
+    adj_copy.start()
     lse_copy = pltpu.make_async_copy(lse_hbm, lse_ref, lse_sem)
     lse_copy.start()
     width = PACK_STEP * HEAD_DIM
@@ -136,6 +138,7 @@
                 [(q_hbm, q_in), (g_hbm, g_in), (o_hbm, o_in), (k_hbm, k_in), (v_hbm, v_in)])])
         for copy in copies[c]:
             copy.start()
+    adj_copy.wait()
     lse_copy.wait()
     for c in range(chunks):
         for copy in copies[c]:
@@ -169,17 +172,17 @@
     shapes = [QROWS, KROWS, QROWS, KROWS, QROWS]
     return pl.pallas_call(
         pack_kernel,
-        in_specs=[smem, smem] + [anywhere] * 6,
+        in_specs=[smem] + [anywhere] * 7,
         out_specs=[spec] * len(shapes),
         out_shape=[vmem((HALF, s, HEAD_DIM), BF16) for s in shapes],
         scratch_shapes=[pltpu.VMEM((BLOCK, 2 * HALF * HEAD_DIM), BF16)] * 5
-        + [pltpu.VMEM((2 * HALF, BLOCK), F32), pltpu.SemaphoreType.DMA((2 * HALF // PACK_STEP, 5)),
-           pltpu.SemaphoreType.DMA],
+        + [pltpu.VMEM((2 * HALF, BLOCK), F32), pltpu.SMEM((1, 2, 1, WINDOW), jnp.int32),
+           pltpu.SemaphoreType.DMA((2 * HALF // PACK_STEP, 5)), pltpu.SemaphoreType.DMA, pltpu.SemaphoreType.DMA],
         compiler_params=pltpu.CompilerParams(vmem_limit_bytes=16 * 2**20),
         cost_estimate=pl.CostEstimate(flops=10**8, bytes_accessed=5 * 2**20, transcendentals=0),
         name="pack",
-    )(odd, adjacency, *[pltpu.with_memory_space_constraint(x, pltpu.HBM)
-                        for x in (row_lse, queries, keys, values, outputs, d_out)])
+    )(odd, *[pltpu.with_memory_space_constraint(x, pltpu.HBM)
+             for x in (adjacency, row_lse, queries, keys, values, outputs, d_out)])
 
 
 Q3 = slice(0, QROWS)
@@ -236,7 +239,7 @@
         far_out[h, 128:256] = dv[128:256].astype(BF16)
         return carry
 
-    lax.fori_loop(0, HALF, one_head, 0)
+    lax.fori_loop(0, HALF, one_head, 0, unroll=4)
 
 
 def attend_b_kernel(odd_ref, xkb, cross, k2, mates, xqb, fq,
@@ -271,7 +274,7 @@
         swap_out[h, 128:256] = dv[384:512].astype(BF16)
         return carry
 
-    lax.fori_loop(0, HALF, one_head, 0)
+    lax.fori_loop(0, HALF, one_head, 0, unroll=4)
 
 
 def block(rows, dtype):
@@ -300,44 +303,56 @@
     return call_on_chip(combine_kernel, name, odd, inputs, [(inputs[0].shape, BF16)], 10**6)[0]
 
 
-def finish_kernel(odd_ref, q_own, kv_a, down, down_sum, far_k, k_own, q_b, up, up_sum, far_q,
-                  dq_hbm, dk_hbm, dv_hbm, dq, dk, dv, sems):
+def finish_kernel(first, grads, outs, stage, sems):
     copies = []
-    for head in range(2 * HALF):
-        h = head % HALF
-        cols = slice(head * HEAD_DIM, (head + 1) * HEAD_DIM)
-        if head < HALF:
-            grad_q = q_own[h] + down_sum[h].astype(F32) + down[h].astype(F32)
-            grad_kv = kv_a[h] + far_k[h].astype(F32)
-        else:
-            grad_q = q_b[h] + far_q[h].astype(F32)
-            grad_kv = k_own[h] + up_sum[h].astype(F32) + up[h].astype(F32)
-        dq[:, cols] = grad_q.astype(BF16)
-        dk[:, cols] = grad_kv[0:128].astype(BF16)
-        dv[:, cols] = grad_kv[128:256].astype(BF16)
-        if head % PACK_STEP == PACK_STEP - 1:
-            c = head // PACK_STEP
-            span = pl.ds(c * PACK_STEP * HEAD_DIM, PACK_STEP * HEAD_DIM)
-            for i, (a, b) in enumerate([(dq, dq_hbm), (dk, dk_hbm), (dv, dv_hbm)]):
-                copies.append(pltpu.make_async_copy(a.at[:, span], b.at[:, span], sems.at[c, i]))
+    step = 2
+    for h in range(HALF):
+        cols = slice(h * HEAD_DIM, (h + 1) * HEAD_DIM)
+        for part, grad in zip(stage, grads(h)):
+            part[:, cols] = grad.astype(BF16)
+        if h % step == step - 1:
+            c = h // step
+            width = step * HEAD_DIM
+            for i, (part, out) in enumerate(zip(stage, outs)):
+                copies.append(pltpu.make_async_copy(
+                    part.at[:, pl.ds(c * width, width)],
+                    out.at[:, pl.ds(first * HEAD_DIM + c * width, width)], sems.at[c, i]))
                 copies[-1].start()
     for copy in copies:
         copy.wait()
 
 
-def finish(odd, *inputs):
+def finish_b_kernel(k_own, q_b, up, up_sum, far_q, dq, dk, dv, *scratch):
+    def grads(h):
+        kv = k_own[h] + up_sum[h].astype(F32) + up[h].astype(F32)
+        return q_b[h] + far_q[h].astype(F32), kv[0:128], kv[128:256]
+
+    finish_kernel(HALF, grads, (dq, dk, dv), scratch[0:3], scratch[3])
+
+
+def finish_a_kernel(q_own, kv_a, down, down_sum, far_k, dq_in, dk_in, dv_in, dq, dk, dv, *scratch):
+    def grads(h):
+        kv = kv_a[h] + far_k[h].astype(F32)
+        return q_own[h] + down_sum[h].astype(F32) + down[h].astype(F32), kv[0:128], kv[128:256]
+
+    finish_kernel(0, grads, (dq, dk, dv), scratch[0:3], scratch[3])
+
+
+def finish(kernel, name, flops, inputs, partial=()):
     spec = pl.BlockSpec(memory_space=pltpu.VMEM)
-    whole = (BLOCK, 2 * HALF * HEAD_DIM)
+    anywhere = pl.BlockSpec(memory_space=pltpu.HBM)
+    whole = jax.ShapeDtypeStruct((BLOCK, 2 * HALF * HEAD_DIM), BF16)
     return pl.pallas_call(
-        finish_kernel,
-        in_specs=[pl.BlockSpec(memory_space=pltpu.SMEM)] + [spec] * len(inputs),
-        out_specs=[pl.BlockSpec(memory_space=pl.ANY)] * 3,
-        out_shape=[jax.ShapeDtypeStruct(whole, BF16)] * 3,
-        scratch_shapes=[pltpu.VMEM(whole, BF16)] * 3 + [pltpu.SemaphoreType.DMA((2 * HALF // PACK_STEP, 3))],
-        compiler_params=pltpu.CompilerParams(vmem_limit_bytes=16 * 2**20),
-        cost_estimate=pl.CostEstimate(flops=10**6, bytes_accessed=6 * 2**20, transcendentals=0),
-        name="finish",
-    )(odd, *[on_chip(x) for x in inputs])
+        kernel,
+        in_specs=[spec] * len(inputs) + [anywhere] * len(partial),
+        out_specs=[anywhere] * 3,
+        out_shape=[whole] * 3,
+        input_output_aliases={len(inputs) + i: i for i in range(len(partial))},
+        scratch_shapes=[pltpu.VMEM((BLOCK, HALF * HEAD_DIM), BF16)] * 3 + [pltpu.SemaphoreType.DMA((HALF // 2, 3))],
+        compiler_params=pltpu.CompilerParams(vmem_limit_bytes=8 * 2**20),
+        cost_estimate=pl.CostEstimate(flops=flops, bytes_accessed=3 * 2**20, transcendentals=0),
+        name=name,
+    )(*[on_chip(x) for x in inputs], *partial)
 
 
 def moved(value, axis, steps):
@@ -381,8 +396,8 @@
     down = crossed(down, -1, -3)
     far_k = moved(far_k, "pb", 1)
     down_sum = moved(combine("combine_a", odd, q_two, exchanged(swap_a)), "ka", -2)
-    here = arrived(odd, far_q, up, up_sum)
-    return tuple(finish(here, q_own, kv_a, down, down_sum, far_k, k_own, q_b, up, up_sum, far_q))
+    grads = finish(finish_b_kernel, "finish_b", WAIT_FLOPS, (k_own, q_b, up, up_sum, far_q))
+    return tuple(finish(finish_a_kernel, "finish_a", 10**6, (q_own, kv_a, down, down_sum, far_k), grads))
 
 
 def solution(mesh):

time: 96.6 us -> 93.6 us (0.969)
  Pallas kernels: 17.4 us -> 13.8 us
  starting transfers between devices: 35.9 us -> 37.1 us
    pallas_call x5, Pallas kernels: 11 us -> 8.3 us  [call_on_chip(): pl.pallas_call(kernel, in_specs=[pl.BlockSpec(memory_space=pltpu.SMEM)] +...]
    ppermute x8, starting transfers between devices: 23.9 us -> 25.1 us  [moved(): lax.ppermute(value, axis, [(i, (i + steps) % count) for i in range(count)])]
    ppermute x8, waiting for transfers between devices: 41.7 us -> 40.7 us  [moved(): lax.ppermute(value, axis, [(i, (i + steps) % count) for i in range(count)])]
    pallas_call x2 -> x3, Pallas kernels: 5.38 us -> 4.99 us  [the longest x1 3.02 us: pack(): pl.pallas_call(pack_kernel, in_specs=[smem] + [anywhere] * 7, out_specs=[...]
  transfers between devices with their start and end apart: 14 -> 14, of which waited for: 6 -> 7; matrix products, arithmetic and copies ran while one was open for 0% -> 0% of each run, Pallas kernels for 12% -> 10%
where the time goes in v2:
time: 93.6 us; the launch traced here: 93.4 us
  waiting for transfers between devices  41.5 us (44%)
  starting transfers between devices  37.1 us (40%)
  Pallas kernels  13.8 us (15%)
    ppermute x8, waiting for transfers between devices, moved(): lax.ppermute(value, axis, [(i, (i + steps) % count) for i in range(count)])  40.7 us
    ppermute x8, starting transfers between devices, moved(): lax.ppermute(value, axis, [(i, (i + steps) % count) for i in range(count)])  25.1 us
    pallas_call x5, Pallas kernels, call_on_chip(): pl.pallas_call(kernel, in_specs=[pl.BlockSpec(memory_space=pltpu.SMEM)] +...  8.3 us
    ppermute x3, starting transfers between devices, exchanged(): return lax.ppermute(value, 'ka', [(i, i ^ 1) for i in range(count)])  7.6 us
    ppermute x3, starting transfers between devices, crossed(): lax.ppermute(value, 'ka', [(i, (i + (odd_steps if i % 2 == 1 else even_st...  4.42 us
    pallas_call x1, Pallas kernels, pack(): pl.pallas_call(pack_kernel, in_specs=[smem] + [anywhere] * 7, out_specs=[...  3.02 us
    pallas_call x2, Pallas kernels, finish(): pl.pallas_call(kernel, in_specs=[spec] * len(inputs) + [anywhere] * len(p...  1.98 us
  transfers between devices with their start and end apart: 14, of which 7 were waited for; matrix products, arithmetic and copies ran while one was open for 0% of the time, Pallas kernels for 10%

profile of v2, /device:TPU:1, one launch (start us, length us, event | category | flops | bytes accessed | tf_op | source)
XLA Modules:
  0.0 93.4 jit_solution(6709016574001751936)
XLA Ops:
  0.6 3.0 %pack.1 = (bf16[8,272,128]{2,1,0:T(8,128)(2,1)S(1)}, bf16[8,256,128]{2,1,0:T(8,128)(2,1)S(1)}, bf16[8,272,128]{2,1,0:T(8,128)(2,1)S(1)}, bf16[8,256,128]{2,1,0:T(8,128)(2,1)S(1)}, bf16[8,272,128]{2,1,0:T(8,128)(2,1)S(1)}) custom-call(s32[1]{0:T(128)} %bitcast.odd_ref, s32[1,2,1,4]{3,2,1,0:T(1,128)} %bitcast.4, f32[16,128]{1,0:T(8,128)} %lse_hbm.1, ...), custom_call_target="tpu_custom_call" | custom-call | flops 100000000 | bytes 5242880 | tf_op jit(solution)/shard_map/pack/pallas_call | solution.py:173
  3.7 2.5 %collective-permute-start.2 = (bf16[8,272,128]{2,1,0:T(8,128)(2,1)S(1)}, bf16[8,272,128]{2,1,0:T(8,128)(2,1)S(1)}, u32[]{:S(2)}, u32[]{:S(2)}) collective-permute-start(bf16[8,272,128]{2,1,0:T(8,128)(2,1)S(1)} %get-tuple-element.35.xqa), channel_id=1, source_target_pairs={{0,2},{1,3},{2,4},{3,5},{4,6},{5,7},{6,8},{7,9},{8,10},{9,11},{10,... | collective-permute-start | bytes 1671176 | tf_op jit(solution)/shard_map/ppermute | solution.py:360
  6.2 2.9 %collective-permute-start = (bf16[8,272,128]{2,1,0:T(8,128)(2,1)S(1)}, bf16[8,272,128]{2,1,0:T(8,128)(2,1)S(1)}, u32[]{:S(2)}, u32[]{:S(2)}) collective-permute-start(bf16[8,272,128]{2,1,0:T(8,128)(2,1)S(1)} %get-tuple-element.33.xqb), channel_id=1, source_target_pairs={{0,32},{32,64},{64,96},{96,128},{128,160},{160,192},{192,224},{224... | collective-permute-start | bytes 1671176 | tf_op jit(solution)/shard_map/ppermute | solution.py:360
  9.1 4.1 %collective-permute-start.1 = (bf16[8,272,128]{2,1,0:T(8,128)(2,1)S(1)}, bf16[8,272,128]{2,1,0:T(8,128)(2,1)S(1)}, u32[]{:S(2)}, u32[]{:S(2)}) collective-permute-start(bf16[8,272,128]{2,1,0:T(8,128)(2,1)S(1)} %get-tuple-element.34), channel_id=1, source_target_pairs={{0,29},{1,4},{2,31},{3,6},{4,1},{5,8},{6,3},{7,10},{8,5},{9,12},{1... | collective-permute-start | bytes 1671176 | tf_op jit(solution)/shard_map/ppermute | solution.py:370
  13.3 1.9 %collective-permute-start.3 = (bf16[8,256,128]{2,1,0:T(8,128)(2,1)S(1)}, bf16[8,256,128]{2,1,0:T(8,128)(2,1)S(1)}, u32[]{:S(2)}, u32[]{:S(2)}) collective-permute-start(bf16[8,256,128]{2,1,0:T(8,128)(2,1)S(1)} %get-tuple-element.36.xkb), channel_id=1, source_target_pairs={{0,30},{1,31},{2,0},{3,1},{4,2},{5,3},{6,4},{7,5},{8,6},{9,7},{10,... | collective-permute-start | bytes 1572872 | tf_op jit(solution)/shard_map/ppermute | solution.py:360
  15.2 17.7 %collective-permute-done.3.k2 = bf16[8,256,128]{2,1,0:T(8,128)(2,1)S(1)} collective-permute-done((bf16[8,256,128]{2,1,0:T(8,128)(2,1)S(1)}, bf16[8,256,128]{2,1,0:T(8,128)(2,1)S(1)}, u32[]{:S(2)}, u32[]{:S(2)}) %collective-permute-start.3) | collective-permute-done | bytes 524320 | tf_op jit(solution)/shard_map/ppermute | solution.py:360
  32.9 0.0 collective-permute-done.2.q2
  32.9 0.1 mates.1
  33.0 6.2 %collective-permute-start.4 = (bf16[8,800,128]{2,1,0:T(8,128)(2,1)S(1)}, bf16[8,800,128]{2,1,0:T(8,128)(2,1)S(1)}, u32[]{:S(2)}, u32[]{:S(2)}) collective-permute-start(bf16[8,800,128]{2,1,0:T(8,128)(2,1)S(1)} %mates.1), channel_id=1, source_target_pairs={{0,1},{1,0},{2,3},{3,2},{4,5},{5,4},{6,7},{7,6},{8,9},{9,8},{10,11... | collective-permute-start | bytes 4915208 | tf_op jit(solution)/shard_map/ppermute | solution.py:365
  39.2 7.1 %collective-permute-start.6 = (bf16[8,256,128]{2,1,0:T(8,128)(2,1)S(1)}, bf16[8,256,128]{2,1,0:T(8,128)(2,1)S(1)}, u32[]{:S(2)}, u32[]{:S(2)}) collective-permute-start(bf16[8,256,128]{2,1,0:T(8,128)(2,1)S(1)} %get-tuple-element.43.xka), channel_id=1, source_target_pairs={{0,224},{32,0},{64,32},{96,64},{128,96},{160,128},{192,160},{224,1... | collective-permute-start | bytes 1572872 | tf_op jit(solution)/shard_map/ppermute | solution.py:360
  46.4 0.0 collective-permute-done.refs_0_.fq
  46.4 0.0 collective-permute-done.1.refs_1_.cross
  46.4 0.5 arrived.1.odd_ref
  46.9 0.0 collective-permute-done.4.mates
  46.9 3.9 %attend_b.1 = (f32[8,256,128]{2,1,0:T(8,128)S(1)}, f32[8,256,128]{2,1,0:T(8,128)S(1)}, f32[8,128,128]{2,1,0:T(8,128)S(1)}, bf16[8,256,128]{2,1,0:T(8,128)(2,1)S(...) custom-call(s32[1]{0:T(128)} %arrived.1.odd_ref, bf16[8,256,128]{2,1,0:T(8,128)(2,1)S(1)} %get-tuple-element.36.xkb, ...), custom_call_target="tpu_custom_call" | custom-call | flops 1300000000 | bytes 4358144 | tf_op jit(solution)/shard_map/attend_b/pallas_call | solution.py:91
  50.9 0.5 collective-permute-start.5
  51.3 2.6 %collective-permute-start.7 = (bf16[8,128,128]{2,1,0:T(8,128)(2,1)S(1)}, bf16[8,128,128]{2,1,0:T(8,128)(2,1)S(1)}, u32[]{:S(2)}, u32[]{:S(2)}) collective-permute-start(bf16[8,128,128]{2,1,0:T(8,128)(2,1)S(1)} %get-tuple-element.50), channel_id=1, source_target_pairs={{0,224},{32,0},{64,32},{96,64},{128,96},{160,128},{192,160},{224,1... | collective-permute-start | bytes 786440 | tf_op jit(solution)/shard_map/ppermute | solution.py:360
  53.9 0.0 collective-permute-start.12
  53.9 4.0 %collective-permute-done.6.fk = bf16[8,256,128]{2,1,0:T(8,128)(2,1)S(1)} collective-permute-done((bf16[8,256,128]{2,1,0:T(8,128)(2,1)S(1)}, bf16[8,256,128]{2,1,0:T(8,128)(2,1)S(1)}, u32[]{:S(2)}, u32[]{:S(2)}) %collective-permute-start.6) | collective-permute-done | bytes 524320 | tf_op jit(solution)/shard_map/ppermute | solution.py:360
  57.9 0.0 collective-permute-done.5.swapped
  57.9 0.1 combine_b.1
  58.0 2.0 %collective-permute-start.13 = (bf16[8,256,128]{2,1,0:T(8,128)(2,1)S(1)}, bf16[8,256,128]{2,1,0:T(8,128)(2,1)S(1)}, u32[]{:S(2)}, u32[]{:S(2)}) collective-permute-start(bf16[8,256,128]{2,1,0:T(8,128)(2,1)S(1)} %combine_b.1), channel_id=1, source_target_pairs={{0,2},{1,3},{2,4},{3,5},{4,6},{5,7},{6,8},{7,9},{8,10},{9,11},{10,... | collective-permute-start | bytes 1572872 | tf_op jit(solution)/shard_map/ppermute | solution.py:360
  60.0 4.0 %attend_a.1 = (f32[8,128,128]{2,1,0:T(8,128)S(1)}, f32[8,128,128]{2,1,0:T(8,128)S(1)}, f32[8,256,128]{2,1,0:T(8,128)S(1)}, bf16[8,128,128]{2,1,0:T(8,128)(2,1)S(...) custom-call(s32[1]{0:T(128)} %arrived.1.odd_ref, bf16[8,272,128]{2,1,0:T(8,128)(2,1)S(1)} %get-tuple-element.35.xqa, ...), custom_call_target="tpu_custom_call" | custom-call | flops 1300000000 | bytes 4358144 | tf_op jit(solution)/shard_map/attend_a/pallas_call | solution.py:91
  64.1 6.5 %collective-permute-done.7.far_q = bf16[8,128,128]{2,1,0:T(8,128)(2,1)S(1)} collective-permute-done((bf16[8,128,128]{2,1,0:T(8,128)(2,1)S(1)}, bf16[8,128,128]{2,1,0:T(8,128)(2,1)S(1)}, u32[]{:S(2)}, u32[]{:S(2)}) %collective-permute-start.7) | collective-permute-done | bytes 262176 | tf_op jit(solution)/shard_map/ppermute | solution.py:360
  70.6 0.9 %collective-permute-start.9 = (bf16[8,128,128]{2,1,0:T(8,128)(2,1)S(1)}, bf16[8,128,128]{2,1,0:T(8,128)(2,1)S(1)}, u32[]{:S(2)}, u32[]{:S(2)}) collective-permute-start(bf16[8,128,128]{2,1,0:T(8,128)(2,1)S(1)} %get-tuple-element.53), channel_id=1, source_target_pairs={{0,1},{1,0},{2,3},{3,2},{4,5},{5,4},{6,7},{7,6},{8,9},{9,8},{10,11... | collective-permute-start | bytes 786440 | tf_op jit(solution)/shard_map/ppermute | solution.py:365
  71.5 5.9 %collective-permute-start.11 = (bf16[8,256,128]{2,1,0:T(8,128)(2,1)S(1)}, bf16[8,256,128]{2,1,0:T(8,128)(2,1)S(1)}, u32[]{:S(2)}, u32[]{:S(2)}) collective-permute-start(bf16[8,256,128]{2,1,0:T(8,128)(2,1)S(1)} %get-tuple-element.54), channel_id=1, source_target_pairs={{0,32},{32,64},{64,96},{96,128},{128,160},{160,192},{192,224},{224... | collective-permute-start | bytes 1572872 | tf_op jit(solution)/shard_map/ppermute | solution.py:360
  77.4 0.3 collective-permute-start.8
  77.7 0.0 collective-permute-done.9.swapped
  77.7 0.1 combine_a.1
  77.8 0.1 collective-permute-start.10
  77.9 0.0 collective-permute-done.12.up
  77.9 4.8 %collective-permute-done.13.up_sum = bf16[8,256,128]{2,1,0:T(8,128)(2,1)S(1)} collective-permute-done((bf16[8,256,128]{2,1,0:T(8,128)(2,1)S(1)}, bf16[8,256,128]{2,1,0:T(8,128)(2,1)S(1)}, u32[]{:S(2)}, u32[]{:S(2)}) %collective-permute-start.13) | collective-permute-done | bytes 524320 | tf_op jit(solution)/shard_map/ppermute | solution.py:360
  82.6 1.0 %finish_b.1 = (bf16[128,2048]{1,0:T(8,128)(2,1)}, bf16[128,2048]{1,0:T(8,128)(2,1)}, bf16[128,2048]{1,0:T(8,128)(2,1)}) custom-call(f32[8,256,128]{2,1,0:T(8,128)S(1)} %get-tuple-element.55.k_own, f32[8,128,128]{2,1,0:T(8,128)S(1)} %get-tuple-element.56.q_b, bf16[8,256,128]{2,1,0:T(8,128)(2,1)S(1)} %collective-permute-done.12.up, ...), custom_call_target="tpu_custom_call" | custom-call | flops 99999997952 | bytes 3145728 | tf_op jit(solution)/shard_map/finish_b/pallas_call | solution.py:345
  83.6 0.8 collective-permute-done.8.down
  84.4 4.2 %collective-permute-done.10.down_sum = bf16[8,128,128]{2,1,0:T(8,128)(2,1)S(1)} collective-permute-done((bf16[8,128,128]{2,1,0:T(8,128)(2,1)S(1)}, bf16[8,128,128]{2,1,0:T(8,128)(2,1)S(1)}, u32[]{:S(2)}, u32[]{:S(2)}) %collective-permute-start.10) | collective-permute-done | bytes 262176 | tf_op jit(solution)/shard_map/ppermute | solution.py:360
  88.6 3.6 %collective-permute-done.11.far_k = bf16[8,256,128]{2,1,0:T(8,128)(2,1)S(1)} collective-permute-done((bf16[8,256,128]{2,1,0:T(8,128)(2,1)S(1)}, bf16[8,256,128]{2,1,0:T(8,128)(2,1)S(1)}, u32[]{:S(2)}, u32[]{:S(2)}) %collective-permute-start.11) | collective-permute-done | bytes 524320 | tf_op jit(solution)/shard_map/ppermute | solution.py:360
  92.2 1.0 %finish_a.1 = (bf16[128,2048]{1,0:T(8,128)(2,1)}, bf16[128,2048]{1,0:T(8,128)(2,1)}, bf16[128,2048]{1,0:T(8,128)(2,1)}) custom-call(f32[8,128,128]{2,1,0:T(8,128)S(1)} %get-tuple-element.45.q_own, f32[8,256,128]{2,1,0:T(8,128)S(1)} %get-tuple-element.46.kv_a, ...), custom_call_target="tpu_custom_call", output_to_operand_aliasing={{0}: (5, {}), {1}: (6, {}), {2}: (7, {})} | custom-call | flops 1000000 | bytes 3145728 | tf_op jit(solution)/shard_map/finish_a/pallas_call | solution.py:345
Async XLA Ops:
  3.7 29.2 %collective-permute-start.2 = (bf16[8,272,128]{2,1,0:T(8,128)(2,1)S(1)}, bf16[8,272,128]{2,1,0:T(8,128)(2,1)S(1)}, u32[]{:S(2)}, u32[]{:S(2)}) collective-permute-start(bf16[8,272,128]{2,1,0:T(8,128)(2,1)S(1)} %get-tuple-element.35.xqa), channel_id=1, source_target_pairs={{0,2},{1,3},{2,4},{3,5},{4,6},{5,7},{6,8},{7,9},{8,10},{9,11},{10,... | collective-permute-start | bytes 1671176 | tf_op jit(solution)/shard_map/ppermute | solution.py:360
  6.2 40.1 %collective-permute-start = (bf16[8,272,128]{2,1,0:T(8,128)(2,1)S(1)}, bf16[8,272,128]{2,1,0:T(8,128)(2,1)S(1)}, u32[]{:S(2)}, u32[]{:S(2)}) collective-permute-start(bf16[8,272,128]{2,1,0:T(8,128)(2,1)S(1)} %get-tuple-element.33.xqb), channel_id=1, source_target_pairs={{0,32},{32,64},{64,96},{96,128},{128,160},{160,192},{192,224},{224... | collective-permute-start | bytes 1671176 | tf_op jit(solution)/shard_map/ppermute | solution.py:360
  9.1 37.2 %collective-permute-start.1 = (bf16[8,272,128]{2,1,0:T(8,128)(2,1)S(1)}, bf16[8,272,128]{2,1,0:T(8,128)(2,1)S(1)}, u32[]{:S(2)}, u32[]{:S(2)}) collective-permute-start(bf16[8,272,128]{2,1,0:T(8,128)(2,1)S(1)} %get-tuple-element.34), channel_id=1, source_target_pairs={{0,29},{1,4},{2,31},{3,6},{4,1},{5,8},{6,3},{7,10},{8,5},{9,12},{1... | collective-permute-start | bytes 1671176 | tf_op jit(solution)/shard_map/ppermute | solution.py:370
  13.3 19.6 %collective-permute-start.3 = (bf16[8,256,128]{2,1,0:T(8,128)(2,1)S(1)}, bf16[8,256,128]{2,1,0:T(8,128)(2,1)S(1)}, u32[]{:S(2)}, u32[]{:S(2)}) collective-permute-start(bf16[8,256,128]{2,1,0:T(8,128)(2,1)S(1)} %get-tuple-element.36.xkb), channel_id=1, source_target_pairs={{0,30},{1,31},{2,0},{3,1},{4,2},{5,3},{6,4},{7,5},{8,6},{9,7},{10,... | collective-permute-start | bytes 1572872 | tf_op jit(solution)/shard_map/ppermute | solution.py:360
  33.0 13.9 %collective-permute-start.4 = (bf16[8,800,128]{2,1,0:T(8,128)(2,1)S(1)}, bf16[8,800,128]{2,1,0:T(8,128)(2,1)S(1)}, u32[]{:S(2)}, u32[]{:S(2)}) collective-permute-start(bf16[8,800,128]{2,1,0:T(8,128)(2,1)S(1)} %mates.1), channel_id=1, source_target_pairs={{0,1},{1,0},{2,3},{3,2},{4,5},{5,4},{6,7},{7,6},{8,9},{9,8},{10,11... | collective-permute-start | bytes 4915208 | tf_op jit(solution)/shard_map/ppermute | solution.py:365
  39.2 18.7 %collective-permute-start.6 = (bf16[8,256,128]{2,1,0:T(8,128)(2,1)S(1)}, bf16[8,256,128]{2,1,0:T(8,128)(2,1)S(1)}, u32[]{:S(2)}, u32[]{:S(2)}) collective-permute-start(bf16[8,256,128]{2,1,0:T(8,128)(2,1)S(1)} %get-tuple-element.43.xka), channel_id=1, source_target_pairs={{0,224},{32,0},{64,32},{96,64},{128,96},{160,128},{192,160},{224,1... | collective-permute-start | bytes 1572872 | tf_op jit(solution)/shard_map/ppermute | solution.py:360
  50.9 7.1 %collective-permute-start.5 = (bf16[8,256,128]{2,1,0:T(8,128)(2,1)S(1)}, bf16[8,256,128]{2,1,0:T(8,128)(2,1)S(1)}, u32[]{:S(2)}, u32[]{:S(2)}) collective-permute-start(bf16[8,256,128]{2,1,0:T(8,128)(2,1)S(1)} %get-tuple-element.41), channel_id=1, source_target_pairs={{0,1},{1,0},{2,3},{3,2},{4,5},{5,4},{6,7},{7,6},{8,9},{9,8},{10,11... | collective-permute-start | bytes 1572872 | tf_op jit(solution)/shard_map/ppermute | solution.py:365
  51.3 19.3 %collective-permute-start.7 = (bf16[8,128,128]{2,1,0:T(8,128)(2,1)S(1)}, bf16[8,128,128]{2,1,0:T(8,128)(2,1)S(1)}, u32[]{:S(2)}, u32[]{:S(2)}) collective-permute-start(bf16[8,128,128]{2,1,0:T(8,128)(2,1)S(1)} %get-tuple-element.50), channel_id=1, source_target_pairs={{0,224},{32,0},{64,32},{96,64},{128,96},{160,128},{192,160},{224,1... | collective-permute-start | bytes 786440 | tf_op jit(solution)/shard_map/ppermute | solution.py:360
  53.9 24.0 %collective-permute-start.12 = (bf16[8,256,128]{2,1,0:T(8,128)(2,1)S(1)}, bf16[8,256,128]{2,1,0:T(8,128)(2,1)S(1)}, u32[]{:S(2)}, u32[]{:S(2)}) collective-permute-start(bf16[8,256,128]{2,1,0:T(8,128)(2,1)S(1)} %get-tuple-element.57), channel_id=1, source_target_pairs={{0,1},{1,4},{2,3},{3,6},{4,5},{5,8},{6,7},{7,10},{8,9},{9,12},{10,... | collective-permute-start | bytes 1572872 | tf_op jit(solution)/shard_map/ppermute | solution.py:370
  58.0 24.6 %collective-permute-start.13 = (bf16[8,256,128]{2,1,0:T(8,128)(2,1)S(1)}, bf16[8,256,128]{2,1,0:T(8,128)(2,1)S(1)}, u32[]{:S(2)}, u32[]{:S(2)}) collective-permute-start(bf16[8,256,128]{2,1,0:T(8,128)(2,1)S(1)} %combine_b.1), channel_id=1, source_target_pairs={{0,2},{1,3},{2,4},{3,5},{4,6},{5,7},{6,8},{7,9},{8,10},{9,11},{10,... | collective-permute-start | bytes 1572872 | tf_op jit(solution)/shard_map/ppermute | solution.py:360
  70.6 7.1 %collective-permute-start.9 = (bf16[8,128,128]{2,1,0:T(8,128)(2,1)S(1)}, bf16[8,128,128]{2,1,0:T(8,128)(2,1)S(1)}, u32[]{:S(2)}, u32[]{:S(2)}) collective-permute-start(bf16[8,128,128]{2,1,0:T(8,128)(2,1)S(1)} %get-tuple-element.53), channel_id=1, source_target_pairs={{0,1},{1,0},{2,3},{3,2},{4,5},{5,4},{6,7},{7,6},{8,9},{9,8},{10,11... | collective-permute-start | bytes 786440 | tf_op jit(solution)/shard_map/ppermute | solution.py:365
  71.5 20.7 %collective-permute-start.11 = (bf16[8,256,128]{2,1,0:T(8,128)(2,1)S(1)}, bf16[8,256,128]{2,1,0:T(8,128)(2,1)S(1)}, u32[]{:S(2)}, u32[]{:S(2)}) collective-permute-start(bf16[8,256,128]{2,1,0:T(8,128)(2,1)S(1)} %get-tuple-element.54), channel_id=1, source_target_pairs={{0,32},{32,64},{64,96},{96,128},{128,160},{160,192},{192,224},{224... | collective-permute-start | bytes 1572872 | tf_op jit(solution)/shard_map/ppermute | solution.py:360
  77.4 7.0 %collective-permute-start.8 = (bf16[8,128,128]{2,1,0:T(8,128)(2,1)S(1)}, bf16[8,128,128]{2,1,0:T(8,128)(2,1)S(1)}, u32[]{:S(2)}, u32[]{:S(2)}) collective-permute-start(bf16[8,128,128]{2,1,0:T(8,128)(2,1)S(1)} %get-tuple-element.51), channel_id=1, source_target_pairs={{0,29},{1,0},{2,31},{3,2},{4,1},{5,4},{6,3},{7,6},{8,5},{9,8},{10,... | collective-permute-start | bytes 786440 | tf_op jit(solution)/shard_map/ppermute | solution.py:370
  77.8 10.8 %collective-permute-start.10 = (bf16[8,128,128]{2,1,0:T(8,128)(2,1)S(1)}, bf16[8,128,128]{2,1,0:T(8,128)(2,1)S(1)}, u32[]{:S(2)}, u32[]{:S(2)}) collective-permute-start(bf16[8,128,128]{2,1,0:T(8,128)(2,1)S(1)} %combine_a.1), channel_id=1, source_target_pairs={{0,30},{1,31},{2,0},{3,1},{4,2},{5,3},{6,4},{7,5},{8,6},{9,7},{10,... | collective-permute-start | bytes 786440 | tf_op jit(solution)/shard_map/ppermute | solution.py:360

commit v3 on v2

--- a/solution.py
+++ b/solution.py
@@ -29,19 +29,19 @@
     return high, middle, rest - middle
 
 
-def pack_head(adj_ref, g, o, lse_row):
-    down = lax.broadcasted_iota(jnp.int32, (BLOCK, BLOCK), 0)
-    across = lax.broadcasted_iota(jnp.int32, (BLOCK, BLOCK), 1)
-    product = contract(o, g, 1, 1)
-    delta_row = jnp.sum(jnp.where(down == across, product, 0.0), axis=0, keepdims=True)
-    rows = list(three_pieces(lse_row)) + list(three_pieces(delta_row))
+def flag_rows(adj_ref):
     line = lax.broadcasted_iota(jnp.int32, (STAT, BLOCK), 0)
     stat = jnp.zeros((STAT, BLOCK), F32)
-    for i, row in enumerate(rows):
-        stat = jnp.where(line == i, jnp.broadcast_to(row, (STAT, BLOCK)), stat)
     for i in range(2 * WINDOW):
         flag = (adj_ref[0, i // WINDOW, 0, i % WINDOW] == 1).astype(jnp.int32).astype(F32)
         stat = jnp.where(line == 8 + i, flag, stat)
+    return line, stat
+
+
+def pack_head(line, stat, diagonal, g, o, lse_row):
+    delta_row = jnp.sum(jnp.where(diagonal, contract(o, g, 1, 1), 0.0), axis=0, keepdims=True)
+    for i, row in enumerate(list(three_pieces(lse_row)) + list(three_pieces(delta_row))):
+        stat = jnp.where(line == i, jnp.broadcast_to(row, (STAT, BLOCK)), stat)
     return stat.astype(BF16)
 
 
@@ -99,22 +99,21 @@
     )(odd, *[on_chip(x) for x in inputs])
 
 
-def arrived_kernel(odd_ref, *refs):
-    refs[-1][0] = odd_ref[0]
-
-
-def arrived(odd, *inputs):
+def arrived_kernel(*refs):
+    refs[-1][...] = jnp.zeros((8, HEAD_DIM), F32)
+
+
+def arrived(*inputs):
     spec = pl.BlockSpec(memory_space=pltpu.VMEM)
-    smem = pl.BlockSpec(memory_space=pltpu.SMEM)
     return pl.pallas_call(
         arrived_kernel,
-        in_specs=[smem] + [spec] * len(inputs),
-        out_specs=smem,
-        out_shape=jax.ShapeDtypeStruct((1,), jnp.int32),
+        in_specs=[spec] * len(inputs),
+        out_specs=spec,
+        out_shape=vmem((8, HEAD_DIM), F32),
         compiler_params=pltpu.CompilerParams(vmem_limit_bytes=2**20),
         cost_estimate=pl.CostEstimate(flops=WAIT_FLOPS, bytes_accessed=2**20, transcendentals=0),
         name="arrived",
-    )(odd, *[on_chip(x) for x in inputs])
+    )(*[on_chip(x) for x in inputs])
 
 
 WAIT_FLOPS = 10**11
@@ -140,6 +139,9 @@
             copy.start()
     adj_copy.wait()
     lse_copy.wait()
+    line, stat = flag_rows(adj_ref)
+    diagonal = (lax.broadcasted_iota(jnp.int32, (BLOCK, BLOCK), 0)
+                == lax.broadcasted_iota(jnp.int32, (BLOCK, BLOCK), 1))
     for c in range(chunks):
         for copy in copies[c]:
             copy.wait()
@@ -149,9 +151,12 @@
             xq, xk = (xqa, xka) if head < HALF else (xqb, xkb)
             xq[h, 0:128, :] = q_in[:, cols]
             xq[h, 128:256, :] = g_in[:, cols]
-            xq[h, 256:272, :] = pack_head(adj_ref, g_in[:, cols], o_in[:, cols], lse_ref[head:head + 1])
+            xq[h, 256:272, :] = pack_head(
+                line, stat, diagonal, g_in[:, cols], o_in[:, cols], lse_ref[head:head + 1])
             xk[h, 0:128, :] = k_in[:, cols]
             xk[h, 128:256, :] = v_in[:, cols]
+            if head >= HALF:
+                xk[h, KROWS:QROWS, :] = jnp.zeros((STAT, HEAD_DIM), BF16)
 
     is_odd = odd_ref[0] == 1
 
@@ -161,15 +166,14 @@
 
     @pl.when(jnp.logical_not(is_odd))
     def _():
-        cross[:, 0:KROWS, :] = xkb[...]
-        cross[:, KROWS:QROWS, :] = jnp.zeros((HALF, STAT, HEAD_DIM), BF16)
+        cross[...] = xkb[...]
 
 
 def pack(odd, adjacency, queries, keys, values, outputs, d_out, row_lse):
     smem = pl.BlockSpec(memory_space=pltpu.SMEM)
     spec = pl.BlockSpec(memory_space=pltpu.VMEM)
     anywhere = pl.BlockSpec(memory_space=pltpu.HBM)
-    shapes = [QROWS, KROWS, QROWS, KROWS, QROWS]
+    shapes = [QROWS, KROWS, QROWS, QROWS, QROWS]
     return pl.pallas_call(
         pack_kernel,
         in_specs=[smem] + [anywhere] * 7,
@@ -195,7 +199,7 @@
 def mates_kernel(odd_ref, xqa, xkb, q2, k2, out):
     def one_head(h, carry):
         out[h, Q3] = q2[h]
-        out[h, K3] = k2[h]
+        out[h, K3] = k2[h, 0:KROWS]
         return carry
 
     lax.fori_loop(0, HALF, one_head, 0)
@@ -203,15 +207,14 @@
 
     @pl.when(is_odd)
     def _():
-        out[:, NEAR_K, :] = xkb[...]
-        out[:, NEAR_K.stop:, :] = jnp.zeros((HALF, STAT, HEAD_DIM), BF16)
+        out[:, NEAR_Q, :] = xkb[...]
 
     @pl.when(jnp.logical_not(is_odd))
     def _():
         out[:, NEAR_Q, :] = xqa[...]
 
 
-def attend_a_kernel(odd_ref, xqa, cross, q2, mates, xka, fk,
+def attend_a_kernel(odd_ref, here, xqa, cross, q2, mates, xka, fk,
                     q_own, q_two, kv_own, swap_out, down_out, far_out):
     odd = odd_ref[0]
     is_odd = odd == 1
@@ -242,7 +245,7 @@
     lax.fori_loop(0, HALF, one_head, 0, unroll=4)
 
 
-def attend_b_kernel(odd_ref, xkb, cross, k2, mates, xqb, fq,
+def attend_b_kernel(odd_ref, here, xkb, cross, k2, mates, xqb, fq,
                     kv_own, kv_two, q_own, swap_out, up_out, far_out):
     odd = odd_ref[0]
     is_odd = odd == 1
@@ -383,15 +386,15 @@
     mates, xka = lax.optimization_barrier((mates, xka))
     mates = exchanged(mates)
     fk = moved(xka, "pb", -1)
-    here = arrived(odd, fq, cross)
-    k_own, k_two, q_b, swap_b, up, far_q = attend_b(here, xkb, cross, k2, mates, xqb, fq)
-    up = crossed(up, 3, 1)
+    here = arrived(fq, cross)
+    k_own, k_two, q_b, swap_b, up, far_q = attend_b(odd, here, xkb, cross, k2, mates, xqb, fq)
     far_q = moved(far_q, "pb", -1)
     swap_b, fk = lax.optimization_barrier((exchanged(swap_b), fk))
     b_sum = combine("combine_b", odd, k_two, swap_b)
-    xka, b_sum = lax.optimization_barrier((xka, b_sum))
+    xka, b_sum, up = lax.optimization_barrier((xka, b_sum, up))
+    up = crossed(up, 3, 1)
     up_sum = moved(b_sum, "ka", 2)
-    q_own, q_two, kv_a, swap_a, down, far_k = attend_a(here, xqa, cross, q2, mates, xka, fk)
+    q_own, q_two, kv_a, swap_a, down, far_k = attend_a(odd, here, xqa, cross, q2, mates, xka, fk)
     down, swap_a, far_k, far_q = lax.optimization_barrier((down, swap_a, far_k, far_q))
     down = crossed(down, -1, -3)
     far_k = moved(far_k, "pb", 1)

time: 93.6 us -> 95.8 us (1.024)
  starting transfers between devices: 37.1 us -> 45.3 us
  waiting for transfers between devices: 41.5 us -> 37.4 us
  Pallas kernels: 13.8 us -> 12.1 us
    ppermute x8, starting transfers between devices: 25.1 us -> 37.6 us  [moved(): lax.ppermute(value, axis, [(i, (i + steps) % count) for i in range(count)])]
    ppermute x3, starting transfers between devices: 4.42 us -> 0.37 us  [crossed(): lax.ppermute(value, 'ka', [(i, (i + (odd_steps if i % 2 == 1 else even_st...]
    ppermute x8, waiting for transfers between devices: 40.7 us -> 37.4 us  [moved(): lax.ppermute(value, axis, [(i, (i + steps) % count) for i in range(count)])]
    pallas_call x5, Pallas kernels: 8.3 us -> 7.06 us  [call_on_chip(): pl.pallas_call(kernel, in_specs=[pl.BlockSpec(memory_space=pltpu.SMEM)] +...]
  transfers between devices with their start and end apart: 14 -> 14, of which waited for: 7 -> 6; matrix products, arithmetic and copies ran while one was open for 0% -> 0% of each run, Pallas kernels for 10% -> 8%
where the time goes in v3:
time: 95.8 us; the launch traced here: 95.7 us
  starting transfers between devices  45.3 us (47%)
  waiting for transfers between devices  37.4 us (39%)
  Pallas kernels  12.1 us (13%)
    ppermute x8, starting transfers between devices, moved(): lax.ppermute(value, axis, [(i, (i + steps) % count) for i in range(count)])  37.6 us
    ppermute x8, waiting for transfers between devices, moved(): lax.ppermute(value, axis, [(i, (i + steps) % count) for i in range(count)])  37.4 us
    ppermute x3, starting transfers between devices, exchanged(): return lax.ppermute(value, 'ka', [(i, i ^ 1) for i in range(count)])  7.37 us
    pallas_call x5, Pallas kernels, call_on_chip(): pl.pallas_call(kernel, in_specs=[pl.BlockSpec(memory_space=pltpu.SMEM)] +...  7.06 us
    pallas_call x1, Pallas kernels, pack(): pl.pallas_call(pack_kernel, in_specs=[smem] + [anywhere] * 7, out_specs=[...  3.02 us
    pallas_call x2, Pallas kernels, finish(): pl.pallas_call(kernel, in_specs=[spec] * len(inputs) + [anywhere] * len(p...  1.99 us
  transfers between devices with their start and end apart: 14, of which 6 were waited for; matrix products, arithmetic and copies ran while one was open for 0% of the time, Pallas kernels for 8%

profile of v3, /device:TPU:1, one launch (start us, length us, event | category | flops | bytes accessed | tf_op | source)
XLA Modules:
  0.0 95.7 jit_solution(15202305323547245762)
XLA Ops:
  0.6 3.0 %pack.1 = (bf16[8,272,128]{2,1,0:T(8,128)(2,1)S(1)}, bf16[8,256,128]{2,1,0:T(8,128)(2,1)S(1)}, bf16[8,272,128]{2,1,0:T(8,128)(2,1)S(1)}, bf16[8,272,128]{2,1,0:T(8,128)(2,1)S(1)}, bf16[8,272,128]{2,1,0:T(8,128)(2,1)S(1)}) custom-call(s32[1]{0:T(128)} %bitcast.odd_ref, s32[1,2,1,4]{3,2,1,0:T(1,128)} %bitcast.4, f32[16,128]{1,0:T(8,128)} %lse_hbm.1, ...), custom_call_target="tpu_custom_call" | custom-call | flops 100000000 | bytes 5242880 | tf_op jit(solution)/shard_map/pack/pallas_call | solution.py:177
  3.7 2.5 %collective-permute-start.2 = (bf16[8,272,128]{2,1,0:T(8,128)(2,1)S(1)}, bf16[8,272,128]{2,1,0:T(8,128)(2,1)S(1)}, u32[]{:S(2)}, u32[]{:S(2)}) collective-permute-start(bf16[8,272,128]{2,1,0:T(8,128)(2,1)S(1)} %get-tuple-element.36.xqa), channel_id=1, source_target_pairs={{0,2},{1,3},{2,4},{3,5},{4,6},{5,7},{6,8},{7,9},{8,10},{9,11},{10,... | collective-permute-start | bytes 1671176 | tf_op jit(solution)/shard_map/ppermute | solution.py:363
  6.2 5.0 %collective-permute-start.3 = (bf16[8,272,128]{2,1,0:T(8,128)(2,1)S(1)}, bf16[8,272,128]{2,1,0:T(8,128)(2,1)S(1)}, u32[]{:S(2)}, u32[]{:S(2)}) collective-permute-start(bf16[8,272,128]{2,1,0:T(8,128)(2,1)S(1)} %get-tuple-element.37.xkb), channel_id=1, source_target_pairs={{0,30},{1,31},{2,0},{3,1},{4,2},{5,3},{6,4},{7,5},{8,6},{9,7},{10,... | collective-permute-start | bytes 1671176 | tf_op jit(solution)/shard_map/ppermute | solution.py:363
  11.3 2.6 %collective-permute-start = (bf16[8,272,128]{2,1,0:T(8,128)(2,1)S(1)}, bf16[8,272,128]{2,1,0:T(8,128)(2,1)S(1)}, u32[]{:S(2)}, u32[]{:S(2)}) collective-permute-start(bf16[8,272,128]{2,1,0:T(8,128)(2,1)S(1)} %get-tuple-element.34.xqb), channel_id=1, source_target_pairs={{0,32},{32,64},{64,96},{96,128},{128,160},{160,192},{192,224},{224... | collective-permute-start | bytes 1671176 | tf_op jit(solution)/shard_map/ppermute | solution.py:363
  13.9 0.0 collective-permute-start.1
  13.9 9.7 %collective-permute-done.2.q2 = bf16[8,272,128]{2,1,0:T(8,128)(2,1)S(1)} collective-permute-done((bf16[8,272,128]{2,1,0:T(8,128)(2,1)S(1)}, bf16[8,272,128]{2,1,0:T(8,128)(2,1)S(1)}, u32[]{:S(2)}, u32[]{:S(2)}) %collective-permute-start.2) | collective-permute-done | bytes 557088 | tf_op jit(solution)/shard_map/ppermute | solution.py:363
  23.5 0.4 collective-permute-done.3.k2
  24.0 0.1 mates.1
  24.1 6.3 %collective-permute-start.4 = (bf16[8,800,128]{2,1,0:T(8,128)(2,1)S(1)}, bf16[8,800,128]{2,1,0:T(8,128)(2,1)S(1)}, u32[]{:S(2)}, u32[]{:S(2)}) collective-permute-start(bf16[8,800,128]{2,1,0:T(8,128)(2,1)S(1)} %mates.1), channel_id=1, source_target_pairs={{0,1},{1,0},{2,3},{3,2},{4,5},{5,4},{6,7},{7,6},{8,9},{9,8},{10,11... | collective-permute-start | bytes 4915208 | tf_op jit(solution)/shard_map/ppermute | solution.py:368
  30.4 15.0 %collective-permute-start.6 = (bf16[8,256,128]{2,1,0:T(8,128)(2,1)S(1)}, bf16[8,256,128]{2,1,0:T(8,128)(2,1)S(1)}, u32[]{:S(2)}, u32[]{:S(2)}) collective-permute-start(bf16[8,256,128]{2,1,0:T(8,128)(2,1)S(1)} %get-tuple-element.45.xka), channel_id=1, source_target_pairs={{0,224},{32,0},{64,32},{96,64},{128,96},{160,128},{192,160},{224,1... | collective-permute-start | bytes 1572872 | tf_op jit(solution)/shard_map/ppermute | solution.py:363
  45.4 0.0 collective-permute-done.refs_0_.fq
  45.4 0.0 collective-permute-done.1.refs_1_.cross
  45.4 0.0 collective-permute-done.4.mates
  45.4 3.3 %attend_b.1 = (f32[8,256,128]{2,1,0:T(8,128)S(1)}, f32[8,256,128]{2,1,0:T(8,128)S(1)}, f32[8,128,128]{2,1,0:T(8,128)S(1)}, bf16[8,256,128]{2,1,0:T(8,128)(2,1)S(...) custom-call(s32[1]{0:T(128)} %bitcast.odd_ref, f32[8,128]{1,0:T(8,128)S(1)} %arrived.1.here, ...), custom_call_target="tpu_custom_call" | custom-call | flops 1300000000 | bytes 4427776 | tf_op jit(solution)/shard_map/attend_b/pallas_call | solution.py:91
  48.7 0.4 collective-permute-start.5
  49.2 5.4 %collective-permute-start.7 = (bf16[8,128,128]{2,1,0:T(8,128)(2,1)S(1)}, bf16[8,128,128]{2,1,0:T(8,128)(2,1)S(1)}, u32[]{:S(2)}, u32[]{:S(2)}) collective-permute-start(bf16[8,128,128]{2,1,0:T(8,128)(2,1)S(1)} %get-tuple-element.52), channel_id=1, source_target_pairs={{0,224},{32,0},{64,32},{96,64},{128,96},{160,128},{192,160},{224,1... | collective-permute-start | bytes 786440 | tf_op jit(solution)/shard_map/ppermute | solution.py:363
  54.5 3.3 %collective-permute-done.6.fk = bf16[8,256,128]{2,1,0:T(8,128)(2,1)S(1)} collective-permute-done((bf16[8,256,128]{2,1,0:T(8,128)(2,1)S(1)}, bf16[8,256,128]{2,1,0:T(8,128)(2,1)S(1)}, u32[]{:S(2)}, u32[]{:S(2)}) %collective-permute-start.6) | collective-permute-done | bytes 524320 | tf_op jit(solution)/shard_map/ppermute | solution.py:363
  57.9 0.0 collective-permute-done.5.swapped
  57.9 0.1 combine_b.1
  58.0 0.1 collective-permute-start.12
  58.1 0.1 collective-permute-start.13
  58.2 3.4 %attend_a.1 = (f32[8,128,128]{2,1,0:T(8,128)S(1)}, f32[8,128,128]{2,1,0:T(8,128)S(1)}, f32[8,256,128]{2,1,0:T(8,128)S(1)}, bf16[8,128,128]{2,1,0:T(8,128)(2,1)S(...) custom-call(s32[1]{0:T(128)} %bitcast.odd_ref, f32[8,128]{1,0:T(8,128)S(1)} %arrived.1.here, ...), custom_call_target="tpu_custom_call" | custom-call | flops 1300000000 | bytes 4362240 | tf_op jit(solution)/shard_map/attend_a/pallas_call | solution.py:91
  61.6 1.9 %collective-permute-done.7.far_q = bf16[8,128,128]{2,1,0:T(8,128)(2,1)S(1)} collective-permute-done((bf16[8,128,128]{2,1,0:T(8,128)(2,1)S(1)}, bf16[8,128,128]{2,1,0:T(8,128)(2,1)S(1)}, u32[]{:S(2)}, u32[]{:S(2)}) %collective-permute-start.7) | collective-permute-done | bytes 262176 | tf_op jit(solution)/shard_map/ppermute | solution.py:363
  63.5 0.7 collective-permute-start.9
  64.1 6.3 %collective-permute-start.11 = (bf16[8,256,128]{2,1,0:T(8,128)(2,1)S(1)}, bf16[8,256,128]{2,1,0:T(8,128)(2,1)S(1)}, u32[]{:S(2)}, u32[]{:S(2)}) collective-permute-start(bf16[8,256,128]{2,1,0:T(8,128)(2,1)S(1)} %get-tuple-element.56), channel_id=1, source_target_pairs={{0,32},{32,64},{64,96},{96,128},{128,160},{160,192},{192,224},{224... | collective-permute-start | bytes 1572872 | tf_op jit(solution)/shard_map/ppermute | solution.py:363
  70.4 0.3 collective-permute-start.8
  70.7 0.0 collective-permute-done.9.swapped
  70.7 0.1 combine_a.1
  70.8 0.6 collective-permute-start.10
  71.4 0.0 collective-permute-done.12.up
  71.4 13.8 %collective-permute-done.13.up_sum = bf16[8,256,128]{2,1,0:T(8,128)(2,1)S(1)} collective-permute-done((bf16[8,256,128]{2,1,0:T(8,128)(2,1)S(1)}, bf16[8,256,128]{2,1,0:T(8,128)(2,1)S(1)}, u32[]{:S(2)}, u32[]{:S(2)}) %collective-permute-start.13) | collective-permute-done | bytes 524320 | tf_op jit(solution)/shard_map/ppermute | solution.py:363
  85.2 1.0 %finish_b.1 = (bf16[128,2048]{1,0:T(8,128)(2,1)}, bf16[128,2048]{1,0:T(8,128)(2,1)}, bf16[128,2048]{1,0:T(8,128)(2,1)}) custom-call(f32[8,256,128]{2,1,0:T(8,128)S(1)} %get-tuple-element.57.k_own, f32[8,128,128]{2,1,0:T(8,128)S(1)} %get-tuple-element.58.q_b, bf16[8,256,128]{2,1,0:T(8,128)(2,1)S(1)} %collective-permute-done.12.up, ...), custom_call_target="tpu_custom_call" | custom-call | flops 99999997952 | bytes 3145728 | tf_op jit(solution)/shard_map/finish_b/pallas_call | solution.py:348
  86.2 0.0 collective-permute-done.8.down
  86.2 0.0 collective-permute-done.10.down_sum
  86.2 8.3 %collective-permute-done.11.far_k = bf16[8,256,128]{2,1,0:T(8,128)(2,1)S(1)} collective-permute-done((bf16[8,256,128]{2,1,0:T(8,128)(2,1)S(1)}, bf16[8,256,128]{2,1,0:T(8,128)(2,1)S(1)}, u32[]{:S(2)}, u32[]{:S(2)}) %collective-permute-start.11) | collective-permute-done | bytes 524320 | tf_op jit(solution)/shard_map/ppermute | solution.py:363
  94.5 1.0 %finish_a.1 = (bf16[128,2048]{1,0:T(8,128)(2,1)}, bf16[128,2048]{1,0:T(8,128)(2,1)}, bf16[128,2048]{1,0:T(8,128)(2,1)}) custom-call(f32[8,128,128]{2,1,0:T(8,128)S(1)} %get-tuple-element.47.q_own, f32[8,256,128]{2,1,0:T(8,128)S(1)} %get-tuple-element.48.kv_a, ...), custom_call_target="tpu_custom_call", output_to_operand_aliasing={{0}: (5, {}), {1}: (6, {}), {2}: (7, {})} | custom-call | flops 1000000 | bytes 3145728 | tf_op jit(solution)/shard_map/finish_a/pallas_call | solution.py:348
  (1 shorter events, 0.0 us)
Async XLA Ops:
  3.7 19.9 %collective-permute-start.2 = (bf16[8,272,128]{2,1,0:T(8,128)(2,1)S(1)}, bf16[8,272,128]{2,1,0:T(8,128)(2,1)S(1)}, u32[]{:S(2)}, u32[]{:S(2)}) collective-permute-start(bf16[8,272,128]{2,1,0:T(8,128)(2,1)S(1)} %get-tuple-element.36.xqa), channel_id=1, source_target_pairs={{0,2},{1,3},{2,4},{3,5},{4,6},{5,7},{6,8},{7,9},{8,10},{9,11},{10,... | collective-permute-start | bytes 1671176 | tf_op jit(solution)/shard_map/ppermute | solution.py:363
  6.2 17.8 %collective-permute-start.3 = (bf16[8,272,128]{2,1,0:T(8,128)(2,1)S(1)}, bf16[8,272,128]{2,1,0:T(8,128)(2,1)S(1)}, u32[]{:S(2)}, u32[]{:S(2)}) collective-permute-start(bf16[8,272,128]{2,1,0:T(8,128)(2,1)S(1)} %get-tuple-element.37.xkb), channel_id=1, source_target_pairs={{0,30},{1,31},{2,0},{3,1},{4,2},{5,3},{6,4},{7,5},{8,6},{9,7},{10,... | collective-permute-start | bytes 1671176 | tf_op jit(solution)/shard_map/ppermute | solution.py:363
  11.3 34.1 %collective-permute-start = (bf16[8,272,128]{2,1,0:T(8,128)(2,1)S(1)}, bf16[8,272,128]{2,1,0:T(8,128)(2,1)S(1)}, u32[]{:S(2)}, u32[]{:S(2)}) collective-permute-start(bf16[8,272,128]{2,1,0:T(8,128)(2,1)S(1)} %get-tuple-element.34.xqb), channel_id=1, source_target_pairs={{0,32},{32,64},{64,96},{96,128},{128,160},{160,192},{192,224},{224... | collective-permute-start | bytes 1671176 | tf_op jit(solution)/shard_map/ppermute | solution.py:363
  13.9 31.5 %collective-permute-start.1 = (bf16[8,272,128]{2,1,0:T(8,128)(2,1)S(1)}, bf16[8,272,128]{2,1,0:T(8,128)(2,1)S(1)}, u32[]{:S(2)}, u32[]{:S(2)}) collective-permute-start(bf16[8,272,128]{2,1,0:T(8,128)(2,1)S(1)} %get-tuple-element.35), channel_id=1, source_target_pairs={{0,29},{1,4},{2,31},{3,6},{4,1},{5,8},{6,3},{7,10},{8,5},{9,12},{1... | collective-permute-start | bytes 1671176 | tf_op jit(solution)/shard_map/ppermute | solution.py:373
  24.1 21.3 %collective-permute-start.4 = (bf16[8,800,128]{2,1,0:T(8,128)(2,1)S(1)}, bf16[8,800,128]{2,1,0:T(8,128)(2,1)S(1)}, u32[]{:S(2)}, u32[]{:S(2)}) collective-permute-start(bf16[8,800,128]{2,1,0:T(8,128)(2,1)S(1)} %mates.1), channel_id=1, source_target_pairs={{0,1},{1,0},{2,3},{3,2},{4,5},{5,4},{6,7},{7,6},{8,9},{9,8},{10,11... | collective-permute-start | bytes 4915208 | tf_op jit(solution)/shard_map/ppermute | solution.py:368
  30.4 27.5 %collective-permute-start.6 = (bf16[8,256,128]{2,1,0:T(8,128)(2,1)S(1)}, bf16[8,256,128]{2,1,0:T(8,128)(2,1)S(1)}, u32[]{:S(2)}, u32[]{:S(2)}) collective-permute-start(bf16[8,256,128]{2,1,0:T(8,128)(2,1)S(1)} %get-tuple-element.45.xka), channel_id=1, source_target_pairs={{0,224},{32,0},{64,32},{96,64},{128,96},{160,128},{192,160},{224,1... | collective-permute-start | bytes 1572872 | tf_op jit(solution)/shard_map/ppermute | solution.py:363
  48.7 9.1 %collective-permute-start.5 = (bf16[8,256,128]{2,1,0:T(8,128)(2,1)S(1)}, bf16[8,256,128]{2,1,0:T(8,128)(2,1)S(1)}, u32[]{:S(2)}, u32[]{:S(2)}) collective-permute-start(bf16[8,256,128]{2,1,0:T(8,128)(2,1)S(1)} %get-tuple-element.42), channel_id=1, source_target_pairs={{0,1},{1,0},{2,3},{3,2},{4,5},{5,4},{6,7},{7,6},{8,9},{9,8},{10,11... | collective-permute-start | bytes 1572872 | tf_op jit(solution)/shard_map/ppermute | solution.py:368
  49.2 14.3 %collective-permute-start.7 = (bf16[8,128,128]{2,1,0:T(8,128)(2,1)S(1)}, bf16[8,128,128]{2,1,0:T(8,128)(2,1)S(1)}, u32[]{:S(2)}, u32[]{:S(2)}) collective-permute-start(bf16[8,128,128]{2,1,0:T(8,128)(2,1)S(1)} %get-tuple-element.52), channel_id=1, source_target_pairs={{0,224},{32,0},{64,32},{96,64},{128,96},{160,128},{192,160},{224,1... | collective-permute-start | bytes 786440 | tf_op jit(solution)/shard_map/ppermute | solution.py:363
  58.0 13.4 %collective-permute-start.12 = (bf16[8,256,128]{2,1,0:T(8,128)(2,1)S(1)}, bf16[8,256,128]{2,1,0:T(8,128)(2,1)S(1)}, u32[]{:S(2)}, u32[]{:S(2)}) collective-permute-start(bf16[8,256,128]{2,1,0:T(8,128)(2,1)S(1)} %get-tuple-element.59), channel_id=1, source_target_pairs={{0,1},{1,4},{2,3},{3,6},{4,5},{5,8},{6,7},{7,10},{8,9},{9,12},{10,... | collective-permute-start | bytes 1572872 | tf_op jit(solution)/shard_map/ppermute | solution.py:373
  58.1 27.1 %collective-permute-start.13 = (bf16[8,256,128]{2,1,0:T(8,128)(2,1)S(1)}, bf16[8,256,128]{2,1,0:T(8,128)(2,1)S(1)}, u32[]{:S(2)}, u32[]{:S(2)}) collective-permute-start(bf16[8,256,128]{2,1,0:T(8,128)(2,1)S(1)} %combine_b.1), channel_id=1, source_target_pairs={{0,2},{1,3},{2,4},{3,5},{4,6},{5,7},{6,8},{7,9},{8,10},{9,11},{10,... | collective-permute-start | bytes 1572872 | tf_op jit(solution)/shard_map/ppermute | solution.py:363
  63.5 7.2 %collective-permute-start.9 = (bf16[8,128,128]{2,1,0:T(8,128)(2,1)S(1)}, bf16[8,128,128]{2,1,0:T(8,128)(2,1)S(1)}, u32[]{:S(2)}, u32[]{:S(2)}) collective-permute-start(bf16[8,128,128]{2,1,0:T(8,128)(2,1)S(1)} %get-tuple-element.55), channel_id=1, source_target_pairs={{0,1},{1,0},{2,3},{3,2},{4,5},{5,4},{6,7},{7,6},{8,9},{9,8},{10,11... | collective-permute-start | bytes 786440 | tf_op jit(solution)/shard_map/ppermute | solution.py:368
  64.1 30.4 %collective-permute-start.11 = (bf16[8,256,128]{2,1,0:T(8,128)(2,1)S(1)}, bf16[8,256,128]{2,1,0:T(8,128)(2,1)S(1)}, u32[]{:S(2)}, u32[]{:S(2)}) collective-permute-start(bf16[8,256,128]{2,1,0:T(8,128)(2,1)S(1)} %get-tuple-element.56), channel_id=1, source_target_pairs={{0,32},{32,64},{64,96},{96,128},{128,160},{160,192},{192,224},{224... | collective-permute-start | bytes 1572872 | tf_op jit(solution)/shard_map/ppermute | solution.py:363
  70.4 15.8 %collective-permute-start.8 = (bf16[8,128,128]{2,1,0:T(8,128)(2,1)S(1)}, bf16[8,128,128]{2,1,0:T(8,128)(2,1)S(1)}, u32[]{:S(2)}, u32[]{:S(2)}) collective-permute-start(bf16[8,128,128]{2,1,0:T(8,128)(2,1)S(1)} %get-tuple-element.53), channel_id=1, source_target_pairs={{0,29},{1,0},{2,31},{3,2},{4,1},{5,4},{6,3},{7,6},{8,5},{9,8},{10,... | collective-permute-start | bytes 786440 | tf_op jit(solution)/shard_map/ppermute | solution.py:373
  70.8 15.4 %collective-permute-start.10 = (bf16[8,128,128]{2,1,0:T(8,128)(2,1)S(1)}, bf16[8,128,128]{2,1,0:T(8,128)(2,1)S(1)}, u32[]{:S(2)}, u32[]{:S(2)}) collective-permute-start(bf16[8,128,128]{2,1,0:T(8,128)(2,1)S(1)} %combine_a.1), channel_id=1, source_target_pairs={{0,30},{1,31},{2,0},{3,1},{4,2},{5,3},{6,4},{7,5},{8,6},{9,7},{10,... | collective-permute-start | bytes 786440 | tf_op jit(solution)/shard_map/ppermute | solution.py:363
